TPU v7x, 32 devices: a whole 2x2x4 slice. The times are simulated.
32 devices in a mesh: row: 8 (over y, x, core), col: 4 (over z).
Axes of the slice: x: 2, y: 2, z: 4, core: 2. Of those that a mesh axis runs over, the one named last changes fastest.
Arguments:
- alignment: float32 [32, 384, 64], P('col', 'row'), may hold values from -6 to 6
- pair_rep: float32 [384, 384, 128], P('row', 'col'), may hold values from -6 to 6
- seq_mask: int32 [32], P('col'), may hold values 0 or 1
- res_mask: int32 [384], P('row'), may hold values 0 or 1
- left_weight: float32 [64, 32], replicated, may hold values from -0.75 to 0.75
- right_weight: float32 [64, 32], replicated, may hold values from -0.75 to 0.75
- w_outer: float32 [1024, 128], replicated, may hold values from -4 to 4
- w_logits: float32 [128, 8], replicated, may hold values from -45 to 45
- value_weight: float32 [64, 256], replicated, may hold values from -0.75 to 0.75
- gate_weight: float32 [64, 256], replicated, may hold values from -0.75 to 0.75
- output_weight: float32 [256, 64], replicated, may hold values from -6 to 6
Outputs:
- alignment_out: float32 [32, 384, 64], P('col', 'row')
- pair_out: float32 [384, 384, 128], P('row', 'col')
All inputs are finite; a program needn't handle non-finite values. No bound on the sum of `seq_mask` or of `res_mask` on one device may be relied on, other than what follows from the above.
Results may differ from a plain program's by a relative error of at most 0.0003.
Values sent between devices are 32-bit elements; how exact they have to be, the bound alone decides.
A program may use at most 128 MiB of HBM per device.

v0:
```python
import functools

import jax
import jax.numpy as jnp
from jax import lax
from jax.experimental import pallas as pl
from jax.experimental.pallas import tpu as pltpu
from jax.sharding import PartitionSpec as P

MESH = pl.DeviceIdType.MESH
F32 = jnp.float32
BF16 = jnp.bfloat16
epsilon = 1e-05
VMEM_LIMIT = 60 * 1024 * 1024


def layer_norm(values):
    center = jnp.mean(values, axis=-1, keepdims=True)
    centred = values - center
    return centred * lax.rsqrt(jnp.mean(centred * centred, axis=-1, keepdims=True) + epsilon)


def split(values):
    high = values.astype(BF16)
    return high, (values - high.astype(F32)).astype(BF16)


def dot(left, right):
    return jnp.dot(left, right, preferred_element_type=F32)


def dot_t(left, right):
    return lax.dot_general(left, right, (((1,), (1,)), ((), ())), preferred_element_type=F32)


def dot_split(left, right_high, right_low, multiply=dot):
    high, low = split(left)
    return multiply(high, right_high) + (multiply(low, right_high) + multiply(high, right_low))


def exchange(
    n_row,
    n_col,
    ratio,
    between,
    seq_ref,
    res_ref,
    align_ref,
    left_w_ref,
    right_w_ref,
    left_out,
    right_out,
    norm_buf,
    rows_buf,
    masked_buf,
    block_buf,
    left_buf,
    right_buf,
    left_send,
    left_recv,
    turn_sem,
    right_send,
    right_recv,
    relay_send,
    relay_recv,
):
    row, col = lax.axis_index("row"), lax.axis_index("col")
    n = n_row * n_col
    me = row * n_col + col
    barrier = pltpu.get_barrier_semaphore()

    def greet(step, carry):
        other = lax.rem(me + step, n)
        pl.semaphore_signal(
            barrier,
            inc=1,
            device_id=(other // n_col, lax.rem(other, n_col)),
            device_id_type=MESH,
        )
        return carry

    lax.fori_loop(1, n, greet, 0)
    seqs, rows, width = align_ref.shape
    res_row = res_ref[...].astype(F32)
    diag = lax.broadcasted_iota(jnp.int32, (rows, rows), 0) == lax.broadcasted_iota(
        jnp.int32, (rows, rows), 1
    )
    res_col = jnp.sum(
        jnp.where(diag, jnp.broadcast_to(res_row, (rows, rows)), 0.0), axis=1, keepdims=True
    )
    factor = right_w_ref.shape[0]
    spread = jnp.broadcast_to(right_w_ref[...][:, None, :], (factor, seqs, width))
    row_seq = lax.broadcasted_iota(jnp.int32, (factor, seqs, width), 1)
    seq_sum = 0.0
    for s in range(seqs):
        normed = layer_norm(align_ref[s])
        norm_buf[:, s * width : (s + 1) * width] = normed
        live = seq_ref[s].astype(F32)
        seq_sum = seq_sum + live
        masked = normed * (res_col * live)
        masked_buf[:, s * width : (s + 1) * width] = masked
        rows_buf[pl.ds(s, rows, stride=seqs), :] = masked
        block_buf[:, s * width : (s + 1) * width] = jnp.where(row_seq == s, spread, 0.0).reshape(
            factor * seqs, width
        )
    wl_high, wl_low = split(left_w_ref[...])
    left = dot_split(rows_buf[...], wl_high, wl_low, dot_t)
    quarter = left.shape[0] // 4
    for g in range(4):
        left_buf[0:quarter, g * factor : (g + 1) * factor] = left[g * quarter : (g + 1) * quarter]
    left_buf[quarter : quarter + 8, :] = jnp.full((8, left_buf.shape[1]), seq_sum, F32)
    wr_high, wr_low = split(block_buf[...])
    right_buf[0:rows, :] = dot_split(masked_buf[...], wr_high, wr_low, dot_t)
    right_buf[rows : rows + 8, 0:rows] = jnp.broadcast_to(res_row, (8, rows))
    right_buf[rows : rows + 8, rows:] = jnp.zeros((8, right_buf.shape[1] - rows), F32)

    pl.semaphore_wait(barrier, n - 1)
    dest = row // ratio
    spot = col * ratio + lax.rem(row, ratio)
    away = dest != col
    half = n_row // 2
    chip, core = row // 2, lax.rem(row, 2)
    partner = 2 * chip + 1 - core

    def peer_row(k):
        return 2 * lax.rem(chip + k, half) + core

    turn = pltpu.make_async_remote_copy(
        right_buf,
        right_out.at[spot],
        turn_sem.at[0],
        turn_sem.at[1],
        device_id=(spot, dest),
        device_id_type=MESH,
    )
    stay = pltpu.make_async_copy(right_buf, right_out.at[spot], turn_sem.at[1])

    @pl.when(away)
    def _():
        turn.start()

    @pl.when(jnp.logical_not(away))
    def _():
        stay.start()

    started = []
    for k in range(1, n_col):
        copy = pltpu.make_async_remote_copy(
            left_buf,
            left_out.at[col],
            left_send.at[k],
            left_recv.at[n_col - k],
            device_id=(row, lax.rem(col + k, n_col)),
            device_id_type=MESH,
        )
        copy.start()
        started.append(copy)
    left_own = pltpu.make_async_copy(left_buf, left_out.at[col], left_recv.at[0])
    left_own.start()
    between()
    pltpu.make_async_copy(right_buf, right_out.at[row], turn_sem.at[1]).wait()
    for k in range(1, half):
        copy = pltpu.make_async_remote_copy(
            right_out.at[row],
            right_out.at[row],
            right_send.at[k],
            right_recv.at[half - k],
            device_id=(peer_row(k), col),
            device_id_type=MESH,
        )
        copy.start()
        started.append(copy)
    for k in range(half):
        src = peer_row(k)
        if k > 0:
            pltpu.make_async_copy(right_buf, right_out.at[src], right_recv.at[k]).wait()
        copy = pltpu.make_async_remote_copy(
            right_out.at[src],
            right_out.at[src],
            relay_send.at[k],
            relay_recv.at[k],
            device_id=(partner, col),
            device_id_type=MESH,
        )
        copy.start()
        started.append(copy)
    left_own.wait()
    for k in range(1, n_col):
        src = lax.rem(col + k, n_col)
        pltpu.make_async_copy(left_buf, left_out.at[src], left_recv.at[k]).wait()
    for k in range(half):
        src = 2 * lax.rem(chip + k, half) + 1 - core
        pltpu.make_async_copy(right_buf, right_out.at[src], relay_recv.at[k]).wait()
    for copy in started:
        copy.wait_send()

    @pl.when(away)
    def _():
        turn.wait_send()


def pair_kernel(
    n_row,
    n_col,
    seq_ref,
    res_ref,
    align_ref,
    left_w_ref,
    right_w_ref,
    outer_ref,
    logits_w_ref,
    pair_ref,
    pair_out,
    slots,
    norm_out,
    w_buf,
    l_buf,
    r_buf,
    mask_buf,
    high_buf,
    low_buf,
    logits_buf,
    logits_send,
    logits_recv,
    logits_own,
    norm_send,
    norm_recv,
    relay_send,
    relay_recv,
    norm_local,
    left_ref,
    right_ref,
    norm_ref,
    *exchange_scratch,
):
    row, col = lax.axis_index("row"), lax.axis_index("col")
    half = n_row // 2
    chip, core = row // 2, lax.rem(row, 2)
    partner = 2 * chip + 1 - core
    quarter = left_ref.shape[1] - 8
    ratio, rows = n_row // n_col, right_ref.shape[1] - 8
    k_col = right_ref.shape[2]
    factor = w_buf.shape[0] // 3
    here, cols, width = pair_ref.shape
    heads = logits_w_ref.shape[0]
    seqs = k_col // factor
    step = pl.program_id(0)
    steps = pl.num_programs(0)

    def peer_row(k):
        return 2 * lax.rem(chip + k, half) + core

    def norm_copy(k):
        return pltpu.make_async_remote_copy(
            norm_ref,
            norm_out.at[row],
            norm_send.at[k],
            norm_recv.at[half - k],
            device_id=(peer_row(k), col),
            device_id_type=MESH,
        )

    def relay_copy(k):
        return pltpu.make_async_remote_copy(
            norm_ref if k == 0 else norm_out.at[peer_row(k)],
            norm_out.at[peer_row(k)],
            relay_send.at[k],
            relay_recv.at[k],
            device_id=(partner, col),
            device_id_type=MESH,
        )

    own_norm = pltpu.make_async_copy(norm_ref, norm_out.at[row], norm_local)
    size = pair_ref.shape[0] * heads

    def logits_copy(k, at):
        part = pl.ds(pl.multiple_of(at * size, size), size)
        return pltpu.make_async_remote_copy(
            logits_buf.at[part],
            slots.at[col, part],
            logits_send.at[k, at],
            logits_recv.at[n_col - k, at],
            device_id=(row, lax.rem(col + k, n_col)),
            device_id_type=MESH,
        )

    def own_logits(at):
        part = pl.ds(pl.multiple_of(at * size, size), size)
        return pltpu.make_async_copy(logits_buf.at[part], slots.at[col, part], logits_own.at[at])

    @pl.when(step == 0)
    def _():
        def between():
            for b in range(factor):
                high, low = split(outer_ref[pl.ds(b, factor, stride=factor), :])
                lanes = slice(b * width, (b + 1) * width)
                w_buf[0:factor, lanes] = high
                w_buf[factor : 2 * factor, lanes] = low
                w_buf[2 * factor : 3 * factor, lanes] = high

        exchange(
            n_row,
            n_col,
            ratio,
            between,
            seq_ref,
            res_ref,
            align_ref,
            left_w_ref,
            right_w_ref,
            left_ref,
            right_ref,
            norm_ref,
            *exchange_scratch,
        )
        own_norm.start()
        count = left_ref[0, quarter : quarter + 1, 0:1]
        for c in range(1, n_col):
            count = count + left_ref[c, quarter : quarter + 1, 0:1]
        scale = 1.0 / jnp.maximum(count, 1.0)
        for c in range(n_col):
            packed = left_ref[c, 0:quarter, :] * scale
            high = packed.astype(BF16).astype(F32)
            low = packed - high
            for g in range(4):
                lanes = slice(g * factor, (g + 1) * factor)
                parts = [high[:, lanes], high[:, lanes], low[:, lanes]]
                l_buf[c, g * quarter : (g + 1) * quarter, :] = jnp.concatenate(
                    parts, axis=1
                ).astype(BF16)
            for t in range(ratio):
                high_r, low_r = split(right_ref[c * ratio + t, 0:rows, :])
                lanes = slice(c * k_col, (c + 1) * k_col)
                r_buf[t * rows : (t + 1) * rows, lanes] = high_r
                r_buf[cols + t * rows : cols + (t + 1) * rows, lanes] = low_r
        for t in range(ratio):
            mask_buf[:, t * rows : (t + 1) * rows] = (
                right_ref[t, rows : rows + 8, 0:rows] - 1.0
            ) * 1000000000.0

    group = here * seqs
    l_rows = jnp.concatenate(
        [l_buf[c, pl.ds(pl.multiple_of(step * group, group), group), :] for c in range(n_col)],
        axis=0,
    )
    for nb in range(factor // 2):
        mixed = dot(l_rows, w_buf[:, nb * 2 * width : (nb + 1) * 2 * width])
        tiles = jnp.concatenate(
            [
                mixed[:, :width].reshape(n_col * here, seqs, width),
                mixed[:, width:].reshape(n_col * here, seqs, width),
            ],
            axis=1,
        )
        high, low = split(tiles)
        for c in range(n_col):
            high_buf[:, c, nb] = high[c * here : (c + 1) * here]
            low_buf[:, c, nb] = low[c * here : (c + 1) * here]
    depth = n_col * k_col
    r_both = r_buf[...]
    w_high, w_low = split(logits_w_ref[...])
    w_both = jnp.concatenate([w_high.astype(F32), w_low.astype(F32)], axis=0).astype(BF16)
    for p in range(here // 2):
        right_high = jnp.concatenate(
            [high_buf[2 * p + t].reshape(depth, width) for t in range(2)], axis=1
        )
        right_low = jnp.concatenate(
            [low_buf[2 * p + t].reshape(depth, width) for t in range(2)], axis=1
        )
        first = dot(r_both, right_high)
        sums = first[:cols] + (first[cols:] + dot(r_both[:cols], right_low))
        for t in range(2):
            i = 2 * p + t
            pair_out[i] = pair_ref[i] + sums[:, t * width : (t + 1) * width]
    batch = here // 2
    for g in range(0, here, batch):
        pairs = pair_out[g : g + batch].reshape(batch * cols, width)
        high, low = split(layer_norm(pairs))
        for t in range(batch):
            one = dot_t(w_both, high[t * cols : (t + 1) * cols])
            two = dot_t(w_both, low[t * cols : (t + 1) * cols])
            logits = one[:heads] + (one[heads:] + two[:heads])
            start = pl.multiple_of(step * size + (g + t) * heads, heads)
            logits_buf[pl.ds(start, heads), :] = logits + mask_buf[...]

    @pl.when(step == 0)
    def _():
        relay_copy(0).start()
        for k in range(1, half):
            norm_copy(k).start()

    for k in range(1, n_col):
        logits_copy(k, step).start()
    own_logits(step).start()

    @pl.when(step == steps // 2)
    def _():
        for k in range(1, half):
            pltpu.make_async_copy(norm_ref, norm_out.at[peer_row(k)], norm_recv.at[k]).wait()
            relay_copy(k).start()

    @pl.when(step == steps - 1)
    def _():
        own_norm.wait()
        for k in range(half):
            other = 2 * lax.rem(chip + k, half) + 1 - core
            relay_copy(k).wait_send()
            pltpu.make_async_copy(norm_ref, norm_out.at[other], relay_recv.at[k]).wait()
        for k in range(1, half):
            norm_copy(k).wait_send()

        def drain(at, carry):
            own_logits(at).wait()
            part = pl.ds(pl.multiple_of(at * size, size), size)
            for k in range(1, n_col):
                logits_copy(k, at).wait_send()
                src = lax.rem(col + k, n_col)
                pltpu.make_async_copy(
                    logits_buf.at[part], slots.at[src, part], logits_recv.at[k, at]
                ).wait()
            return carry

        lax.fori_loop(0, steps, drain, 0)


def average_kernel(
    slots,
    norm_ref,
    align_ref,
    value_w_ref,
    gate_w_ref,
    output_w_ref,
    pair_ref,
    out_ref,
    pair_out,
    terms_buf,
    pair_buf,
    pair_sem,
):
    bring = pltpu.make_async_copy(pair_ref, pair_buf, pair_sem.at[0])
    bring.start()
    seqs, rows, width = align_ref.shape
    n_col, total_rows, cols = slots.shape
    heads = total_rows // rows
    channels = value_w_ref.shape[1]
    head_width = channels // heads
    wv_high, wv_low = split(value_w_ref[...])
    wg_high, wg_low = split(gate_w_ref[...])
    wo_high, wo_low = split(output_w_ref[...])
    own_head = (
        lax.broadcasted_iota(jnp.int32, (heads, channels), 1) // head_width
        == lax.broadcasted_iota(jnp.int32, (heads, channels), 0)
    ).astype(F32)
    top = jnp.max(slots[0], axis=1, keepdims=True)
    for c in range(1, n_col):
        top = jnp.maximum(top, jnp.max(slots[c], axis=1, keepdims=True))
    total = jnp.zeros_like(top)
    for c in range(n_col):
        terms = jnp.exp(slots[c] - top)
        terms_buf[c] = terms
        total = total + jnp.sum(terms, axis=1, keepdims=True)
    inverse = 1.0 / total
    mixed = None
    for c in range(n_col):
        high, low = split(norm_ref[c * cols : (c + 1) * cols, :])
        part = dot_split(terms_buf[c] * inverse, high, low)
        mixed = part if mixed is None else mixed + part
    bring.wait()
    place = pltpu.make_async_copy(pair_buf, pair_out, pair_sem.at[1])
    place.start()
    for s in range(seqs):
        wide = dot_split(mixed[:, s * width : (s + 1) * width], wv_high, wv_low)
        averaged = jnp.sum(wide.reshape(rows, heads, channels) * own_head[None], axis=1)
        align = align_ref[s]
        gate = jax.nn.sigmoid(dot_split(layer_norm(align), wg_high, wg_low))
        out_ref[s] = align + dot_split(gate * averaged, wo_high, wo_low, dot_t)
    place.wait()


def per_device(
    n_row,
    n_col,
    alignment,
    pair_rep,
    seq_mask,
    res_mask,
    left_weight,
    right_weight,
    w_outer,
    w_logits,
    value_weight,
    gate_weight,
    output_weight,
):
    seqs, rows, width = alignment.shape
    cols, pair_width = pair_rep.shape[1], pair_rep.shape[2]
    factor = left_weight.shape[1]
    heads = w_logits.shape[1]
    ratio = cols // rows
    k_col = factor * seqs
    quarter = rows * seqs // 4
    half = n_row // 2
    vmem = pl.BlockSpec(memory_space=pltpu.VMEM)
    smem = pl.BlockSpec(memory_space=pltpu.SMEM)
    dma = pltpu.SemaphoreType.DMA
    left_shape = (quarter + 8, 4 * factor)
    right_shape = (rows + 8, k_col)
    norm_shape = (rows, seqs * width)
    here = 8
    steps = rows // here
    anywhere = pl.BlockSpec(memory_space=pl.ANY)
    full = lambda shape: pl.BlockSpec(shape, lambda i: (0,) * len(shape), pipeline_mode=pl.Buffered(1))
    pair_out, slots, norm_all = pl.pallas_call(
        functools.partial(pair_kernel, n_row, n_col),
        grid=(steps,),
        out_shape=(
            jax.ShapeDtypeStruct(pair_rep.shape, F32),
            jax.ShapeDtypeStruct((n_col, rows * heads, cols), F32),
            jax.ShapeDtypeStruct((n_row,) + norm_shape, F32),
        ),
        in_specs=[
            smem,
            vmem,
            vmem,
            vmem,
            vmem,
            full(w_outer.shape),
            full((heads, pair_width)),
            pl.BlockSpec((here, cols, pair_width), lambda i: (i, 0, 0)),
        ],
        out_specs=(
            pl.BlockSpec((here, cols, pair_width), lambda i: (i, 0, 0)),
            anywhere,
            anywhere,
        ),
        scratch_shapes=[
            pltpu.VMEM((3 * factor, factor * pair_width), BF16),
            pltpu.VMEM((n_col, rows * seqs, 3 * factor), BF16),
            pltpu.VMEM((2 * cols, n_col * k_col), BF16),
            pltpu.VMEM((8, cols), F32),
            pltpu.VMEM((here, n_col, factor // 2, 2 * seqs, pair_width), BF16),
            pltpu.VMEM((here, n_col, factor // 2, 2 * seqs, pair_width), BF16),
            pltpu.VMEM((rows * heads, cols), F32),
            dma((n_col, steps)),
            dma((n_col, steps)),
            dma((steps,)),
            dma((half,)),
            dma((half,)),
            dma((half,)),
            dma((half,)),
            dma,
            pltpu.VMEM((n_col,) + left_shape, F32),
            pltpu.VMEM((n_row,) + right_shape, F32),
            pltpu.VMEM(norm_shape, F32),
            pltpu.VMEM((rows * seqs, width), F32),
            pltpu.VMEM(norm_shape, F32),
            pltpu.VMEM((k_col, seqs * width), F32),
            pltpu.VMEM(left_shape, F32),
            pltpu.VMEM(right_shape, F32),
            dma((n_col,)),
            dma((n_col,)),
            dma((2,)),
            dma((half,)),
            dma((half,)),
            dma((half,)),
            dma((half,)),
        ],
        compiler_params=pltpu.CompilerParams(
            collective_id=0, has_side_effects=True, vmem_limit_bytes=VMEM_LIMIT
        ),
        name="pair",
    )(
        seq_mask,
        res_mask.reshape(1, rows),
        alignment,
        left_weight.T,
        right_weight.T,
        w_outer,
        w_logits.T,
        pair_rep,
    )
    alignment_out, pair_final = pl.pallas_call(
        average_kernel,
        out_shape=(
            jax.ShapeDtypeStruct(alignment.shape, F32),
            jax.ShapeDtypeStruct(pair_rep.shape, F32),
        ),
        in_specs=[vmem] * 6 + [anywhere],
        out_specs=(vmem, anywhere),
        scratch_shapes=[
            pltpu.VMEM(slots.shape, F32),
            pltpu.VMEM(pair_rep.shape, F32),
            dma((2,)),
        ],
        compiler_params=pltpu.CompilerParams(vmem_limit_bytes=VMEM_LIMIT),
        name="average",
    )(
        slots,
        norm_all.reshape(n_row * rows, seqs * width),
        alignment,
        value_weight,
        gate_weight,
        output_weight.T,
        pair_out,
    )
    return (alignment_out, pair_final)


def solution(mesh):
    in_specs = (P("col", "row", None), P("row", "col", None), P("col"), P("row")) + (P(),) * 7
    out_specs = (P("col", "row", None), P("row", "col", None))
    return jax.shard_map(
        functools.partial(per_device, mesh.shape["row"], mesh.shape["col"]),
        mesh=mesh,
        in_specs=in_specs,
        out_specs=out_specs,
        check_vma=False,
    )
```

profile of v0, /device:TPU:0, one launch (start us, length us, event | category | flops | bytes accessed | tf_op | source)
XLA Modules:
  0.0 50.4 jit_solution(17031582840984384055)
XLA Ops:
  0.6 42.0 %pair.1 = (f32[48,96,128]{2,1,0:T(8,128)}, f32[4,384,96]{2,1,0:T(8,128)}, f32[8,48,512]{2,1,0:T(8,128)}) custom-call(s32[8]{0:T(128)} %seq_ref.1, s32[1,48]{1,0:T(1,128)} %bitcast.11, f32[8,48,64]{2,1,0:T(8,128)} %align_ref.3, f32[32,64]{1,0:T(8,128)} %bitcast.8, f32[32,64]{1,0:T(8,128)} %bitcast.9, f32[1024,128]{1,0:T(8,128)} %outer_ref.1, ...), custom_call_target="tpu_custom_call" | custom-call | tf_op jit(solution)/shard_map/pair/pallas_call | solution.py:513
  42.7 7.7 %average.1 = (f32[8,48,64]{2,1,0:T(8,128)}, f32[48,96,128]{2,1,0:T(8,128)}) custom-call(f32[4,384,96]{2,1,0:T(8,128)} %get-tuple-element.5.slots, f32[384,512]{1,0:T(8,128)} %bitcast.6, f32[8,48,64]{2,1,0:T(8,128)} %align_ref.3, f32[64,256]{1,0:T(8,128)} %value_w_ref.1, f32[64,256]{1,0:T(8,128)} %gate_w_ref.1, f32[64,256]{1,0:T(8,128)} %bitcast.7, ...), custom_call_target="tpu_custom_call" | custom-call | tf_op jit(solution)/shard_map/average/pallas_call | solution.py:582
where the time goes:
time: 50.6 us; the launch traced here: 50.4 us
  Pallas kernels  49.8 us (98%)
  between operations  0.64 us (1%)
    pallas_call x1, Pallas kernels, per_device(): pl.pallas_call(functools.partial(pair_kernel, n_row, n_col), grid=(steps,...  42 us
    pallas_call x1, Pallas kernels, per_device(): pl.pallas_call(average_kernel, out_shape=(jax.ShapeDtypeStruct(alignment....  7.74 us

commit v1 on v0

v1 whole, which is shorter than its diff:
```python
import functools

import jax
import jax.numpy as jnp
from jax import lax
from jax.experimental import pallas as pl
from jax.experimental.pallas import tpu as pltpu
from jax.sharding import PartitionSpec as P

MESH = pl.DeviceIdType.MESH
F32 = jnp.float32
BF16 = jnp.bfloat16
epsilon = 1e-05
PAIR_VMEM = 48 * 1024 * 1024
AVERAGE_VMEM = 24 * 1024 * 1024
MIX_BYTES = 30 * 1024 * 1024
LANES = 128


def layer_norm(values):
    center = jnp.mean(values, axis=-1, keepdims=True)
    centred = values - center
    return centred * lax.rsqrt(jnp.mean(centred * centred, axis=-1, keepdims=True) + epsilon)


def split(values):
    high = values.astype(BF16)
    return high, (values - high.astype(F32)).astype(BF16)


def dot(left, right):
    return jnp.dot(left, right, preferred_element_type=F32)


def dot_t(left, right):
    return lax.dot_general(left, right, (((1,), (1,)), ((), ())), preferred_element_type=F32)


def t_dot(left, right):
    return lax.dot_general(left, right, (((0,), (0,)), ((), ())), preferred_element_type=F32)


def dot_split(left, right_high, right_low, multiply=dot):
    high, low = split(left)
    return multiply(high, right_high) + (multiply(low, right_high) + multiply(high, right_low))


def iota(shape, axis):
    return lax.broadcasted_iota(jnp.int32, shape, axis)


def stacked_dot(values, weights):
    count, half = values.shape[0], weights.shape[1] // 2
    high, low = split(values)
    out = dot(jnp.concatenate([high, low], axis=0), weights)
    out = out[:, :half] + out[:, half:]
    return out[:count] + out[count:]


def spread_heads(weight, heads, group, store):
    width, channels = weight.shape
    head_width = channels // heads
    both = jnp.concatenate(split(weight), axis=0)
    rows, lanes = iota((channels, LANES), 0), iota((channels, LANES), 1)
    own = iota((group * width, LANES), 0) // width == iota((group * width, LANES), 1) // head_width
    for h in range(heads):
        pick = jnp.where(rows == h * head_width + lanes % head_width, 1.0, 0.0).astype(BF16)
        tiled = dot(both, pick)
        parts = []
        for t in range(2):
            piece = jnp.concatenate([tiled[t * width : (t + 1) * width]] * group, axis=0)
            parts.append(jnp.where(own, piece, 0.0))
        store(h, jnp.concatenate(parts, axis=1).astype(BF16))


def pair_kernel(
    n_row,
    n_col,
    here,
    seq_in,
    res_in,
    align_in,
    left_w_in,
    right_w_in,
    outer_in,
    logits_w_in,
    value_w_in,
    gate_w_in,
    output_w_in,
    pair_in,
    pair_out,
    slots,
    norm_all,
    gate_out,
    value_bd,
    output_bd,
    align_ref,
    seq_ref,
    res_ref,
    left_w_ref,
    right_w_ref,
    outer_ref,
    logits_w_ref,
    value_w_ref,
    gate_w_ref,
    output_w_ref,
    rows_buf,
    masked_buf,
    block_buf,
    right_buf,
    left_ref,
    right_ref,
    gate_bd,
    wl_buf,
    w_buf,
    l_buf,
    r_buf,
    mask_buf,
    high_buf,
    low_buf,
    load_sem,
    left_send,
    left_recv,
    turn_sem,
    right_send,
    right_recv,
    share_send,
    share_recv,
    logits_send,
    logits_recv,
    norm_send,
    norm_recv,
    relay_send,
    relay_recv,
):
    row, col = lax.axis_index("row"), lax.axis_index("col")
    n = n_row * n_col
    me = row * n_col + col
    barrier = pltpu.get_barrier_semaphore()
    loads = [
        pltpu.make_async_copy(source, target, load_sem.at[at])
        for at, (source, target) in enumerate(
            [
                (align_in, align_ref),
                (seq_in, seq_ref),
                (res_in, res_ref),
                (right_w_in, right_w_ref),
                (left_w_in, left_w_ref),
                (outer_in, outer_ref),
                (gate_w_in, gate_w_ref),
                (value_w_in, value_w_ref),
                (logits_w_in, logits_w_ref),
                (output_w_in, output_w_ref),
                (pair_in, pair_out),
            ]
        )
    ]
    for load in loads:
        load.start()

    def greet(step, carry):
        other = lax.rem(me + step, n)
        pl.semaphore_signal(
            barrier,
            inc=1,
            device_id=(other // n_col, lax.rem(other, n_col)),
            device_id_type=MESH,
        )
        return carry

    lax.fori_loop(1, n, greet, 0)

    seqs, rows, width = align_ref.shape
    factor = right_w_ref.shape[0]
    ratio, k_col = n_row // n_col, factor * seqs
    half = n_row // 2
    chip, core = row // 2, lax.rem(row, 2)
    partner = 2 * chip + 1 - core
    cols, pair_width = pair_out.shape[1], pair_out.shape[2]
    heads = logits_w_ref.shape[0]
    quarter = rows * seqs // 4
    steps = rows // here
    parts = LANES // (here * heads)
    jrows = cols // parts
    group = LANES * heads // value_w_ref.shape[1]
    premixed = high_buf.shape[0] == rows
    depth = n_col * k_col

    def peer_row(k):
        return 2 * lax.rem(chip + k, half) + core

    relayed = n_col >= 4
    at_high, at_low = col == n_col - 2, col == 1
    relay = at_high | at_low
    far_src = jnp.where(at_low, n_col - 1, 0)
    far_dest = jnp.where(at_low, 0, n_col - 1)

    def is_far(other):
        return (other - col == n_col - 1) | (col - other == n_col - 1)

    def near(other, action):
        if relayed:
            pl.when(jnp.logical_not(is_far(other)))(action)
        else:
            action()

    def unless_relayed(src, action):
        if relayed:
            pl.when(jnp.logical_not(relay & (src == far_src)))(action)
        else:
            action()

    for at in range(5):
        loads[at].wait()
    res_row = res_ref[...].astype(F32)
    diag = iota((rows, rows), 0) == iota((rows, rows), 1)

    def column(values):
        return jnp.sum(
            jnp.where(diag, jnp.broadcast_to(values, (rows, rows)), 0.0), axis=1, keepdims=True
        )

    res_col = column(res_row)
    spread = jnp.broadcast_to(right_w_ref[...][:, None, :], (factor, seqs, width))
    row_seq = iota((factor, seqs, width), 1)
    seq_sum = 0.0
    for s in range(seqs):
        normed = layer_norm(align_ref[s])
        norm_all[row, :, s * width : (s + 1) * width] = normed
        live = seq_ref[s].astype(F32)
        seq_sum = seq_sum + live
        masked = normed * (res_col * live)
        masked_buf[:, s * width : (s + 1) * width] = masked
        rows_buf[pl.ds(s, rows, stride=seqs), :] = masked
        block_buf[:, s * width : (s + 1) * width] = jnp.where(row_seq == s, spread, 0.0).reshape(
            factor * seqs, width
        )
    wr_high, wr_low = split(block_buf[...])
    right_buf[0:rows, :] = dot_split(masked_buf[...], wr_high, wr_low, dot_t)
    right_buf[rows : rows + 8, 0:rows] = jnp.broadcast_to(res_row, (8, rows))
    right_buf[rows : rows + 8, rows:] = jnp.zeros((8, right_buf.shape[1] - rows), F32)
    wl_high, wl_low = split(left_w_ref[...])
    left = dot_split(rows_buf[...], wl_high, wl_low, dot_t)
    for g in range(4):
        left_ref[col, 0:quarter, g * factor : (g + 1) * factor] = left[
            g * quarter : (g + 1) * quarter
        ]
    left_ref[col, quarter : quarter + 8, :] = jnp.full((8, left_ref.shape[2]), seq_sum, F32)

    pl.semaphore_wait(barrier, n - 1)
    dest = row // ratio
    spot = col * ratio + lax.rem(row, ratio)
    away = dest != col
    turn = pltpu.make_async_remote_copy(
        right_buf,
        right_ref.at[spot],
        turn_sem.at[0],
        turn_sem.at[1],
        device_id=(spot, dest),
        device_id_type=MESH,
    )
    stay = pltpu.make_async_copy(right_buf, right_ref.at[spot], turn_sem.at[1])

    @pl.when(away)
    def _():
        turn.start()

    @pl.when(jnp.logical_not(away))
    def _():
        stay.start()

    def left_copy(k):
        return pltpu.make_async_remote_copy(
            left_ref.at[col],
            left_ref.at[col],
            left_send.at[k],
            left_recv.at[col],
            device_id=(row, lax.rem(col + k, n_col)),
            device_id_type=MESH,
        )

    def left_forward():
        return pltpu.make_async_remote_copy(
            left_ref.at[far_src],
            left_ref.at[far_src],
            left_send.at[0],
            left_recv.at[far_src],
            device_id=(row, far_dest),
            device_id_type=MESH,
        )

    def left_wait(src):
        pltpu.make_async_copy(left_ref.at[src], left_ref.at[src], left_recv.at[src]).wait()

    for k in range(1, n_col):
        near(lax.rem(col + k, n_col), left_copy(k).start)

    def right_copy(k):
        return pltpu.make_async_remote_copy(
            right_ref.at[row],
            right_ref.at[row],
            right_send.at[k],
            right_recv.at[half - k],
            device_id=(peer_row(k), col),
            device_id_type=MESH,
        )

    def share_copy(k):
        src = peer_row(k)
        return pltpu.make_async_remote_copy(
            right_ref.at[src],
            right_ref.at[src],
            share_send.at[k],
            share_recv.at[k],
            device_id=(partner, col),
            device_id_type=MESH,
        )

    def norm_copy(k):
        return pltpu.make_async_remote_copy(
            norm_all.at[row],
            norm_all.at[row],
            norm_send.at[k],
            norm_recv.at[half - k],
            device_id=(peer_row(k), col),
            device_id_type=MESH,
        )

    def relay_copy(k):
        return pltpu.make_async_remote_copy(
            norm_all.at[peer_row(k)],
            norm_all.at[peer_row(k)],
            relay_send.at[k],
            relay_recv.at[k],
            device_id=(partner, col),
            device_id_type=MESH,
        )

    loads[5].wait()
    for b in range(factor):
        high, low = split(outer_ref[pl.ds(b, factor, stride=factor), :])
        lanes = slice(b * pair_width, (b + 1) * pair_width)
        w_buf[0:factor, lanes] = high
        w_buf[factor : 2 * factor, lanes] = low
        w_buf[2 * factor : 3 * factor, lanes] = high

    def left_rows(c, at):
        packed = left_ref[c, 0:quarter, :]
        high = packed.astype(BF16).astype(F32)
        low = packed - high
        for g in range(4):
            lanes = slice(g * factor, (g + 1) * factor)
            pieces = [high[:, lanes], high[:, lanes], low[:, lanes]]
            l_buf[at, g * quarter : (g + 1) * quarter, :] = jnp.concatenate(
                pieces, axis=1
            ).astype(BF16)

    def mix(l_rows, c, count):
        for nb in range(factor // 2):
            mixed = dot(l_rows, w_buf[:, nb * 2 * pair_width : (nb + 1) * 2 * pair_width])
            tiles = jnp.concatenate(
                [
                    mixed[:, :pair_width].reshape(count, seqs, pair_width),
                    mixed[:, pair_width:].reshape(count, seqs, pair_width),
                ],
                axis=1,
            )
            high, low = split(tiles)
            high_buf[:, c, nb] = high
            low_buf[:, c, nb] = low

    def prepare():
        for at in range(6, 11):
            loads[at].wait()

        def keep_value(h, block):
            value_bd[h] = block

        def keep_gate(h, block):
            gate_bd[h] = block

        spread_heads(gate_w_ref[...], heads, group, keep_gate)
        spread_heads(value_w_ref[...], heads, group, keep_value)
        for g in range(seqs // group):
            own = norm_all[row, :, g * group * width : (g + 1) * group * width]
            for h in range(heads):
                gate_out[g, h] = jax.nn.sigmoid(stacked_dot(own, gate_bd[h]))
        channels = output_w_ref.shape[1]
        head_width = channels // heads
        lanes = iota((width, group * width), 1)
        pick = jnp.where(iota((width, group * width), 0) == lanes % width, 1.0, 0.0).astype(BF16)
        own = (iota((2 * group * head_width, group * width), 0) // head_width) % group == iota(
            (2 * group * head_width, group * width), 1
        ) // width
        for t, half_w in enumerate(split(output_w_ref[...])):
            tiled = t_dot(half_w, pick)
            for hp in range(heads // 2):
                pieces = []
                for hh in range(2):
                    first = (2 * hp + hh) * head_width
                    pieces += [tiled[first : first + head_width]] * group
                output_bd[t, hp] = jnp.where(own, jnp.concatenate(pieces, axis=0), 0.0).astype(BF16)
        lanes = iota((heads, 2 * LANES), 1)
        low_half = iota((pair_width, 2 * LANES), 1) >= LANES
        w_high, w_low = split(logits_w_ref[...])
        for i in range(here):
            pick = jnp.where(
                ((lanes // here) % heads == iota((heads, 2 * LANES), 0)) & (lanes % here == i),
                1.0,
                0.0,
            ).astype(BF16)
            block = jnp.where(low_half, t_dot(w_low, pick), t_dot(w_high, pick))
            wl_buf[i // 2, (i % 2) * pair_width : (i % 2 + 1) * pair_width, :] = block.astype(BF16)

    low_end = col < (n_col + 1) // 2
    spot_in = jnp.where(low_end, col, n_col - 1 - col)

    def stage(k, carry):
        order = jnp.where(k - 1 < spot_in, k - 1, k)
        src = jnp.where(low_end, order, n_col - 1 - order)
        src = jnp.where(k == 0, col, src)

        @pl.when(k == 1)
        def _():
            prepare()
            pltpu.make_async_copy(right_buf, right_ref.at[row], turn_sem.at[1]).wait()
            for k2 in range(1, half):
                right_copy(k2).start()
            share_copy(0).start()
            if relayed:

                @pl.when(relay)
                def _():
                    left_wait(far_src)
                    left_forward().start()

        @pl.when(k == n_col - 1)
        def _():
            for k2 in range(1, half):
                pltpu.make_async_copy(
                    right_buf, right_ref.at[peer_row(k2)], right_recv.at[k2]
                ).wait()
                share_copy(k2).start()
            relay_copy(0).start()
            for k2 in range(1, half):
                norm_copy(k2).start()

        @pl.when(k > 0)
        def _():
            unless_relayed(src, lambda: left_wait(src))

        at = 0 if premixed else src
        left_rows(src, at)
        if premixed:
            mix(l_buf[0], src, rows)
        return carry

    lax.fori_loop(0, n_col, stage, 0)
    for k in range(half):
        src = 2 * lax.rem(chip + k, half) + 1 - core
        pltpu.make_async_copy(right_buf, right_ref.at[src], share_recv.at[k]).wait()
    count = left_ref[0, quarter : quarter + 1, 0:1]
    for c in range(1, n_col):
        count = count + left_ref[c, quarter : quarter + 1, 0:1]
    scale = 1.0 / jnp.maximum(count, 1.0)
    for c in range(n_col):
        for t in range(ratio):
            high_r, low_r = split(right_ref[c * ratio + t, 0:rows, :])
            lanes = slice(c * k_col, (c + 1) * k_col)
            r_buf[t * rows : (t + 1) * rows, lanes] = high_r
            r_buf[cols + t * rows : cols + (t + 1) * rows, lanes] = low_r
    res_cols = jnp.concatenate(
        [column(right_ref[t, rows : rows + 1, 0:rows]) for t in range(ratio)], axis=0
    )
    part_of = iota((jrows, LANES), 1) // (here * heads)
    mask = jnp.zeros((jrows, LANES), F32)
    for p in range(parts):
        dead = (res_cols[p * jrows : (p + 1) * jrows] - 1.0) * 1000000000.0
        mask = jnp.where(part_of == p, dead, mask)
    mask_buf[...] = mask

    def chunk(at):
        return pl.ds(pl.multiple_of(at * jrows, jrows), jrows)

    def logits_copy(k, at):
        return pltpu.make_async_remote_copy(
            slots.at[col, chunk(at)],
            slots.at[col, chunk(at)],
            logits_send.at[k, at],
            logits_recv.at[col, at],
            device_id=(row, lax.rem(col + k, n_col)),
            device_id_type=MESH,
        )

    def logits_forward(at):
        return pltpu.make_async_remote_copy(
            slots.at[far_src, chunk(at)],
            slots.at[far_src, chunk(at)],
            logits_send.at[0, at],
            logits_recv.at[far_src, at],
            device_id=(row, far_dest),
            device_id_type=MESH,
        )

    def logits_wait(src, at):
        pltpu.make_async_copy(
            slots.at[src, chunk(at)], slots.at[src, chunk(at)], logits_recv.at[src, at]
        ).wait()

    def pass_on(at):
        @pl.when(relay)
        def _():
            logits_wait(far_src, at)
            logits_forward(at).start()

    lag = 2

    def body(step, carry):
        first_row = pl.multiple_of(step * here, here)
        if not premixed:
            size = here * seqs
            for c in range(n_col):
                mix(l_buf[c, pl.ds(pl.multiple_of(step * size, size), size), :], c, here)
        r_both = r_buf[...]
        total = None
        for p in range(here // 2):
            at = [2 * p + t + (first_row if premixed else 0) for t in range(2)]
            right_high = jnp.concatenate(
                [high_buf[i].reshape(depth, pair_width) for i in at], axis=1
            )
            right_low = jnp.concatenate([low_buf[i].reshape(depth, pair_width) for i in at], axis=1)
            first = dot(r_both, right_high)
            sums = first[:cols] + (first[cols:] + dot(r_both[:cols], right_low))
            high, low = [], []
            for t in range(2):
                i = first_row + 2 * p + t
                pair = pair_out[i] + sums[:, t * pair_width : (t + 1) * pair_width] * scale
                pair_out[i] = pair
                pieces = split(layer_norm(pair))
                high.append(pieces[0])
                low.append(pieces[1])
            both = jnp.concatenate(
                [jnp.concatenate(high, axis=1), jnp.concatenate(low, axis=1)], axis=0
            )
            out = dot(both, wl_buf[p])
            out = out[:, :LANES] + out[:, LANES:]
            out = out[:cols] + out[cols:]
            total = out if total is None else total + out
        logits = total[:jrows]
        for p in range(1, parts):
            logits = jnp.where(part_of == p, total[p * jrows : (p + 1) * jrows], logits)
        slots[col, chunk(step), :] = logits + mask_buf[...]
        for k in range(1, n_col):
            near(lax.rem(col + k, n_col), logits_copy(k, step).start)
        if relayed:

            @pl.when(step >= lag)
            def _():
                pass_on(step - lag)

        @pl.when(step == steps // 2)
        def _():
            for k in range(1, half):
                pltpu.make_async_copy(
                    norm_all.at[row], norm_all.at[peer_row(k)], norm_recv.at[k]
                ).wait()
                relay_copy(k).start()

        return carry

    lax.fori_loop(0, steps, body, 0)
    if relayed:
        for at in range(steps - lag, steps):
            pass_on(at)
    for k in range(half):
        other = 2 * lax.rem(chip + k, half) + 1 - core
        pltpu.make_async_copy(norm_all.at[row], norm_all.at[other], relay_recv.at[k]).wait()
        relay_copy(k).wait_send()
        share_copy(k).wait_send()
    for k in range(1, half):
        norm_copy(k).wait_send()
        right_copy(k).wait_send()
    for k in range(1, n_col):
        near(lax.rem(col + k, n_col), left_copy(k).wait_send)

    @pl.when(away)
    def _():
        turn.wait_send()

    if relayed:

        @pl.when(relay)
        def _():
            left_forward().wait_send()

    def drain(at, carry):
        for k in range(1, n_col):
            other = lax.rem(col + k, n_col)
            near(other, logits_copy(k, at).wait_send)
            unless_relayed(other, lambda: logits_wait(other, at))
        if relayed:

            @pl.when(relay)
            def _():
                logits_forward(at).wait_send()

        return carry

    lax.fori_loop(0, steps, drain, 0)


def average_kernel(
    here,
    slots,
    norm_ref,
    gate_ref,
    value_bd,
    output_bd,
    align_ref,
    pair_ref,
    out_any,
    pair_any,
    out_buf,
    sems,
):
    place = pltpu.make_async_copy(pair_ref, pair_any, sems.at[0])
    place.start()
    seqs, rows, width = align_ref.shape
    n_col, total_rows, _ = slots.shape
    groups, heads = gate_ref.shape[0], gate_ref.shape[1]
    group = seqs // groups
    steps = rows // here
    jrows = total_rows // steps
    wide = here * heads
    parts = LANES // wide
    norm_high, norm_low = split(norm_ref[...])
    part_of = iota((jrows, LANES), 1) // wide

    def over_parts(values, combine):
        out = values
        for p in range(1, parts):
            out = combine(out, pltpu.roll(values, p * wide, 1))
        return out

    weights = []
    for t in range(steps):
        pieces = [slots[c, t * jrows : (t + 1) * jrows, :] for c in range(n_col)]
        top = pieces[0]
        for piece in pieces[1:]:
            top = jnp.maximum(top, piece)
        top = over_parts(jnp.max(top, axis=0, keepdims=True), jnp.maximum)
        pieces = [jnp.exp(piece - top) for piece in pieces]
        total = pieces[0]
        for piece in pieces[1:]:
            total = total + piece
        inverse = 1.0 / over_parts(jnp.sum(total, axis=0, keepdims=True), jnp.add)
        weights.append([piece * inverse for piece in pieces])
    turned = []
    for t in range(0, steps, parts):
        blocks = []
        for c in range(n_col):
            for p in range(parts):
                block = None
                for q in range(parts):
                    value = weights[t + q][c]
                    shift = (q - p) % parts * wide
                    if shift:
                        value = pltpu.roll(value, shift, 1)
                    block = value if block is None else jnp.where(part_of == q, value, block)
                blocks.append(block)
        turned.append(jnp.concatenate(blocks, axis=0).T)
    mixed = dot_split(jnp.concatenate(turned, axis=0), norm_high, norm_low)
    for g in range(groups):
        gated = []
        for h in range(heads):
            own = jnp.concatenate(
                [
                    mixed[
                        t * wide + h * here : t * wide + (h + 1) * here,
                        g * group * width : (g + 1) * group * width,
                    ]
                    for t in range(steps)
                ],
                axis=0,
            )
            gated.append(stacked_dot(own, value_bd[h]) * gate_ref[g, h])
        out = None
        for hp in range(heads // 2):
            part = dot_split(
                jnp.concatenate(gated[2 * hp : 2 * hp + 2], axis=1),
                output_bd[0, hp],
                output_bd[1, hp],
            )
            out = part if out is None else out + part
        for s in range(group):
            at = g * group + s
            out_buf[at] = align_ref[at] + out[:, s * width : (s + 1) * width]
        pltpu.make_async_copy(
            out_buf.at[pl.ds(g * group, group)],
            out_any.at[pl.ds(g * group, group)],
            sems.at[1 + g],
        ).start()
    for g in range(groups):
        pltpu.make_async_copy(
            out_buf.at[pl.ds(g * group, group)],
            out_any.at[pl.ds(g * group, group)],
            sems.at[1 + g],
        ).wait()
    place.wait()


def per_device(
    n_row,
    n_col,
    alignment,
    pair_rep,
    seq_mask,
    res_mask,
    left_weight,
    right_weight,
    w_outer,
    w_logits,
    value_weight,
    gate_weight,
    output_weight,
):
    seqs, rows, width = alignment.shape
    cols, pair_width = pair_rep.shape[1], pair_rep.shape[2]
    factor = left_weight.shape[1]
    heads = w_logits.shape[1]
    channels = value_weight.shape[1]
    k_col = factor * seqs
    quarter = rows * seqs // 4
    half = n_row // 2
    here = 8
    steps = rows // here
    jrows = cols * here * heads // LANES
    group = LANES * heads // channels
    groups = seqs // group
    vmem = pl.BlockSpec(memory_space=pltpu.VMEM)
    anywhere = pl.BlockSpec(memory_space=pl.ANY)
    dma = pltpu.SemaphoreType.DMA
    left_shape = (quarter + 8, 4 * factor)
    right_shape = (rows + 8, k_col)
    mix_row = (n_col, factor // 2, 2 * seqs, pair_width)
    row_bytes = 4 * n_col * k_col * pair_width
    premixed = rows * row_bytes <= MIX_BYTES
    held = rows if premixed else here
    pair_new, slots, norm_all, gate, value_bd, output_bd, align = pl.pallas_call(
        functools.partial(pair_kernel, n_row, n_col, here),
        out_shape=(
            pltpu.VMEM(pair_rep.shape, F32),
            pltpu.VMEM((n_col, steps * jrows, LANES), F32),
            pltpu.VMEM((n_row, rows, seqs * width), F32),
            pltpu.VMEM((groups, heads, rows, LANES), F32),
            pltpu.VMEM((heads, group * width, 2 * LANES), BF16),
            pltpu.VMEM((2, heads // 2, 2 * LANES, group * width), BF16),
            pltpu.VMEM(alignment.shape, F32),
        ),
        in_specs=[anywhere] * 11,
        out_specs=(vmem,) * 7,
        scratch_shapes=[
            pltpu.SMEM((seqs,), jnp.int32),
            pltpu.VMEM((1, rows), jnp.int32),
            pltpu.VMEM((factor, width), F32),
            pltpu.VMEM((factor, width), F32),
            pltpu.VMEM(w_outer.shape, F32),
            pltpu.VMEM((heads, pair_width), F32),
            pltpu.VMEM(value_weight.shape, F32),
            pltpu.VMEM(gate_weight.shape, F32),
            pltpu.VMEM((width, channels), F32),
            pltpu.VMEM((rows * seqs, width), F32),
            pltpu.VMEM((rows, seqs * width), F32),
            pltpu.VMEM((k_col, seqs * width), F32),
            pltpu.VMEM(right_shape, F32),
            pltpu.VMEM((n_col,) + left_shape, F32),
            pltpu.VMEM((n_row,) + right_shape, F32),
            pltpu.VMEM((heads, group * width, 2 * LANES), BF16),
            pltpu.VMEM((here // 2, 2 * pair_width, 2 * LANES), BF16),
            pltpu.VMEM((3 * factor, factor * pair_width), BF16),
            pltpu.VMEM((1 if premixed else n_col, rows * seqs, 3 * factor), BF16),
            pltpu.VMEM((2 * cols, n_col * k_col), BF16),
            pltpu.VMEM((jrows, LANES), F32),
            pltpu.VMEM((held,) + mix_row, BF16),
            pltpu.VMEM((held,) + mix_row, BF16),
            dma((11,)),
            dma((n_col,)),
            dma((n_col,)),
            dma((2,)),
            dma((half,)),
            dma((half,)),
            dma((half,)),
            dma((half,)),
            dma((n_col, steps)),
            dma((n_col, steps)),
            dma((half,)),
            dma((half,)),
            dma((half,)),
            dma((half,)),
        ],
        compiler_params=pltpu.CompilerParams(
            collective_id=0, has_side_effects=True, vmem_limit_bytes=PAIR_VMEM
        ),
        name="pair",
    )(
        seq_mask,
        res_mask.reshape(1, rows),
        alignment,
        left_weight.T,
        right_weight.T,
        w_outer,
        w_logits.T,
        value_weight,
        gate_weight,
        output_weight.T,
        pair_rep,
    )
    alignment_out, pair_final = pl.pallas_call(
        functools.partial(average_kernel, here),
        out_shape=(
            jax.ShapeDtypeStruct(alignment.shape, F32),
            jax.ShapeDtypeStruct(pair_rep.shape, F32),
        ),
        in_specs=[vmem] * 7,
        out_specs=(anywhere, anywhere),
        scratch_shapes=[pltpu.VMEM(alignment.shape, F32), dma((1 + groups,))],
        compiler_params=pltpu.CompilerParams(vmem_limit_bytes=AVERAGE_VMEM),
        name="average",
    )(
        slots,
        norm_all.reshape(n_row * rows, seqs * width),
        gate,
        value_bd,
        output_bd,
        align,
        pair_new,
    )
    return (alignment_out, pair_final)


def solution(mesh):
    in_specs = (P("col", "row", None), P("row", "col", None), P("col"), P("row")) + (P(),) * 7
    out_specs = (P("col", "row", None), P("row", "col", None))
    return jax.shard_map(
        functools.partial(per_device, mesh.shape["row"], mesh.shape["col"]),
        mesh=mesh,
        in_specs=in_specs,
        out_specs=out_specs,
        check_vma=False,
    )
```

time: 50.6 us -> 47.3 us (0.935)
  Pallas kernels: 49.8 us -> 46.6 us
    pallas_call x2, Pallas kernels: 49.8 us -> 46.6 us  [the longest x1 43 us: per_device(): pl.pallas_call(functools.partial(pair_kernel, n_row, n_col, here), out_sh...]
where the time goes in v1:
time: 47.3 us; the launch traced here: 47.2 us
  Pallas kernels  46.6 us (99%)
  between operations  0.64 us (1%)
    pallas_call x1, Pallas kernels, per_device(): pl.pallas_call(functools.partial(pair_kernel, n_row, n_col, here), out_sh...  43 us
    pallas_call x1, Pallas kernels, per_device(): pl.pallas_call(functools.partial(average_kernel, here), out_shape=(jax.Sh...  3.55 us

profile of v1, /device:TPU:0, one launch (start us, length us, event | category | flops | bytes accessed | tf_op | source)
XLA Modules:
  0.0 47.2 jit_solution(8115301490291612004)
XLA Ops:
  0.6 43.0 %pair.1 = (f32[48,96,128]{2,1,0:T(8,128)S(1)}, f32[4,288,128]{2,1,0:T(8,128)S(1)}, f32[8,48,512]{2,1,0:T(8,128)S(1)}, f32[2,8,48,128]{3,2,1,0:T(8,128)S(1)}, bf1...) custom-call(s32[8]{0:T(128)} %seq_in.1, s32[1,48]{1,0:T(1,128)} %bitcast.11, ...), custom_call_target="tpu_custom_call" | custom-call | tf_op jit(solution)/shard_map/pair/pallas_call | solution.py:749
  43.6 3.5 %average.1 = (f32[8,48,64]{2,1,0:T(8,128)}, f32[48,96,128]{2,1,0:T(8,128)}) custom-call(f32[4,288,128]{2,1,0:T(8,128)S(1)} %get-tuple-element.9.slots, f32[384,512]{1,0:T(8,128)S(1)} %bitcast.6, f32[2,8,48,128]{3,2,1,0:T(8,128)S(1)} %get-tuple-element.11.gate_ref, bf16[8,256,256]{2,1,0:T(8,128)(2,1)S(1)} %get-tuple-element.12.value_bd, ...), custom_call_target="tpu_custom_call" | custom-call | tf_op jit(solution)/shard_map/average/pallas_call | solution.py:818

commit v2 on v1

--- a/solution.py
+++ b/solution.py
@@ -118,6 +118,7 @@
     mask_buf,
     high_buf,
     low_buf,
+    pair_ref,
     load_sem,
     left_send,
     left_recv,
@@ -151,7 +152,7 @@
                 (value_w_in, value_w_ref),
                 (logits_w_in, logits_w_ref),
                 (output_w_in, output_w_ref),
-                (pair_in, pair_out),
+                (pair_in, pair_ref),
             ]
         )
     ]
@@ -522,7 +523,6 @@
             for c in range(n_col):
                 mix(l_buf[c, pl.ds(pl.multiple_of(step * size, size), size), :], c, here)
         r_both = r_buf[...]
-        total = None
         for p in range(here // 2):
             at = [2 * p + t + (first_row if premixed else 0) for t in range(2)]
             right_high = jnp.concatenate(
@@ -531,21 +531,32 @@
             right_low = jnp.concatenate([low_buf[i].reshape(depth, pair_width) for i in at], axis=1)
             first = dot(r_both, right_high)
             sums = first[:cols] + (first[cols:] + dot(r_both[:cols], right_low))
-            high, low = [], []
             for t in range(2):
                 i = first_row + 2 * p + t
-                pair = pair_out[i] + sums[:, t * pair_width : (t + 1) * pair_width] * scale
-                pair_out[i] = pair
-                pieces = split(layer_norm(pair))
-                high.append(pieces[0])
-                low.append(pieces[1])
-            both = jnp.concatenate(
-                [jnp.concatenate(high, axis=1), jnp.concatenate(low, axis=1)], axis=0
-            )
-            out = dot(both, wl_buf[p])
-            out = out[:, :LANES] + out[:, LANES:]
-            out = out[:cols] + out[cols:]
-            total = out if total is None else total + out
+                pair_out[i] = pair_ref[i] + sums[:, t * pair_width : (t + 1) * pair_width] * scale
+        total = None
+        batch = here // 2
+        for g in range(0, here, batch):
+            pairs = pair_out[pl.ds(first_row + g, batch)].reshape(batch * cols, pair_width)
+            high, low = split(layer_norm(pairs))
+            for p in range(batch // 2):
+                both = jnp.concatenate(
+                    [
+                        jnp.concatenate(
+                            [
+                                half_x[(2 * p + t) * cols : (2 * p + t + 1) * cols]
+                                for t in range(2)
+                            ],
+                            axis=1,
+                        )
+                        for half_x in (high, low)
+                    ],
+                    axis=0,
+                )
+                out = dot(both, wl_buf[g // 2 + p])
+                out = out[:, :LANES] + out[:, LANES:]
+                out = out[:cols] + out[cols:]
+                total = out if total is None else total + out
         logits = total[:jrows]
         for p in range(1, parts):
             logits = jnp.where(part_of == p, total[p * jrows : (p + 1) * jrows], logits)
@@ -783,6 +794,7 @@
             pltpu.VMEM((jrows, LANES), F32),
             pltpu.VMEM((held,) + mix_row, BF16),
             pltpu.VMEM((held,) + mix_row, BF16),
+            pltpu.VMEM(pair_rep.shape, F32),
             dma((11,)),
             dma((n_col,)),
             dma((n_col,)),

time: 47.3 us -> 38.6 us (0.82)
  Pallas kernels: 46.6 us -> 37.8 us
    pallas_call x1, Pallas kernels: 43 us -> 34.3 us  [per_device(): pl.pallas_call(functools.partial(pair_kernel, n_row, n_col, here), out_sh...]
where the time goes in v2:
time: 38.6 us; the launch traced here: 38.5 us
  Pallas kernels  37.8 us (98%)
  between operations  0.64 us (2%)
    pallas_call x1, Pallas kernels, per_device(): pl.pallas_call(functools.partial(pair_kernel, n_row, n_col, here), out_sh...  34.3 us
    pallas_call x1, Pallas kernels, per_device(): pl.pallas_call(functools.partial(average_kernel, here), out_shape=(jax.Sh...  3.55 us

profile of v2, /device:TPU:0, one launch (start us, length us, event | category | flops | bytes accessed | tf_op | source)
XLA Modules:
  0.0 38.5 jit_solution(15514684864149075483)
XLA Ops:
  0.6 34.3 %pair.1 = (f32[48,96,128]{2,1,0:T(8,128)S(1)}, f32[4,288,128]{2,1,0:T(8,128)S(1)}, f32[8,48,512]{2,1,0:T(8,128)S(1)}, f32[2,8,48,128]{3,2,1,0:T(8,128)S(1)}, bf1...) custom-call(s32[8]{0:T(128)} %seq_in.1, s32[1,48]{1,0:T(1,128)} %bitcast.11, ...), custom_call_target="tpu_custom_call" | custom-call | tf_op jit(solution)/shard_map/pair/pallas_call | solution.py:760
  34.9 3.5 %average.1 = (f32[8,48,64]{2,1,0:T(8,128)}, f32[48,96,128]{2,1,0:T(8,128)}) custom-call(f32[4,288,128]{2,1,0:T(8,128)S(1)} %get-tuple-element.9.slots, f32[384,512]{1,0:T(8,128)S(1)} %bitcast.6, f32[2,8,48,128]{3,2,1,0:T(8,128)S(1)} %get-tuple-element.11.gate_ref, bf16[8,256,256]{2,1,0:T(8,128)(2,1)S(1)} %get-tuple-element.12.value_bd, ...), custom_call_target="tpu_custom_call" | custom-call | tf_op jit(solution)/shard_map/average/pallas_call | solution.py:830

commit v3 on v2

--- a/solution.py
+++ b/solution.py
@@ -135,8 +135,6 @@
     relay_recv,
 ):
     row, col = lax.axis_index("row"), lax.axis_index("col")
-    n = n_row * n_col
-    me = row * n_col + col
     barrier = pltpu.get_barrier_semaphore()
     loads = [
         pltpu.make_async_copy(source, target, load_sem.at[at])
@@ -159,18 +157,6 @@
     for load in loads:
         load.start()
 
-    def greet(step, carry):
-        other = lax.rem(me + step, n)
-        pl.semaphore_signal(
-            barrier,
-            inc=1,
-            device_id=(other // n_col, lax.rem(other, n_col)),
-            device_id_type=MESH,
-        )
-        return carry
-
-    lax.fori_loop(1, n, greet, 0)
-
     seqs, rows, width = align_ref.shape
     factor = right_w_ref.shape[0]
     ratio, k_col = n_row // n_col, factor * seqs
@@ -211,6 +197,28 @@
         else:
             action()
 
+    dest = row // ratio
+    spot = col * ratio + lax.rem(row, ratio)
+    away = dest != col
+
+    def meet(action):
+        for k in range(1, n_col):
+            other = lax.rem(col + k, n_col)
+            near(other, functools.partial(action, row, other))
+        for k in range(1, half):
+            action(peer_row(k), col)
+        action(partner, col)
+        pl.when(away)(functools.partial(action, spot, dest))
+
+    def greet(other_row, other_col):
+        pl.semaphore_signal(
+            barrier, inc=1, device_id=(other_row, other_col), device_id_type=MESH
+        )
+
+    greeters = half + n_col - 1 + jnp.where(away, 1, 0)
+    if relayed:
+        greeters = greeters - jnp.where((col == 0) | (col == n_col - 1), 1, 0)
+    meet(greet)
     for at in range(5):
         loads[at].wait()
     res_row = res_ref[...].astype(F32)
@@ -240,18 +248,7 @@
     right_buf[0:rows, :] = dot_split(masked_buf[...], wr_high, wr_low, dot_t)
     right_buf[rows : rows + 8, 0:rows] = jnp.broadcast_to(res_row, (8, rows))
     right_buf[rows : rows + 8, rows:] = jnp.zeros((8, right_buf.shape[1] - rows), F32)
-    wl_high, wl_low = split(left_w_ref[...])
-    left = dot_split(rows_buf[...], wl_high, wl_low, dot_t)
-    for g in range(4):
-        left_ref[col, 0:quarter, g * factor : (g + 1) * factor] = left[
-            g * quarter : (g + 1) * quarter
-        ]
-    left_ref[col, quarter : quarter + 8, :] = jnp.full((8, left_ref.shape[2]), seq_sum, F32)
-
-    pl.semaphore_wait(barrier, n - 1)
-    dest = row // ratio
-    spot = col * ratio + lax.rem(row, ratio)
-    away = dest != col
+    pl.semaphore_wait(barrier, greeters)
     turn = pltpu.make_async_remote_copy(
         right_buf,
         right_ref.at[spot],
@@ -270,6 +267,14 @@
     def _():
         stay.start()
 
+    wl_high, wl_low = split(left_w_ref[...])
+    left = dot_split(rows_buf[...], wl_high, wl_low, dot_t)
+    for g in range(4):
+        left_ref[col, 0:quarter, g * factor : (g + 1) * factor] = left[
+            g * quarter : (g + 1) * quarter
+        ]
+    left_ref[col, quarter : quarter + 8, :] = jnp.full((8, left_ref.shape[2]), seq_sum, F32)
+
     def left_copy(k):
         return pltpu.make_async_remote_copy(
             left_ref.at[col],
@@ -292,9 +297,6 @@
 
     def left_wait(src):
         pltpu.make_async_copy(left_ref.at[src], left_ref.at[src], left_recv.at[src]).wait()
-
-    for k in range(1, n_col):
-        near(lax.rem(col + k, n_col), left_copy(k).start)
 
     def right_copy(k):
         return pltpu.make_async_remote_copy(
@@ -423,6 +425,8 @@
 
         @pl.when(k == 1)
         def _():
+            for k2 in range(1, n_col):
+                near(lax.rem(col + k2, n_col), left_copy(k2).start)
             prepare()
             pltpu.make_async_copy(right_buf, right_ref.at[row], turn_sem.at[1]).wait()
             for k2 in range(1, half):
@@ -514,7 +518,7 @@
             logits_wait(far_src, at)
             logits_forward(at).start()
 
-    lag = 2
+    lag, direct = 2, 1
 
     def body(step, carry):
         first_row = pl.multiple_of(step * here, here)
@@ -562,7 +566,13 @@
             logits = jnp.where(part_of == p, total[p * jrows : (p + 1) * jrows], logits)
         slots[col, chunk(step), :] = logits + mask_buf[...]
         for k in range(1, n_col):
-            near(lax.rem(col + k, n_col), logits_copy(k, step).start)
+            other = lax.rem(col + k, n_col)
+            if relayed:
+                pl.when(jnp.logical_not(is_far(other)) | (step >= steps - direct))(
+                    logits_copy(k, step).start
+                )
+            else:
+                logits_copy(k, step).start()
         if relayed:
 
             @pl.when(step >= lag)
@@ -581,7 +591,7 @@
 
     lax.fori_loop(0, steps, body, 0)
     if relayed:
-        for at in range(steps - lag, steps):
+        for at in range(steps - lag, steps - direct):
             pass_on(at)
     for k in range(half):
         other = 2 * lax.rem(chip + k, half) + 1 - core
@@ -617,7 +627,12 @@
 
         return carry
 
-    lax.fori_loop(0, steps, drain, 0)
+    if relayed:
+        lax.fori_loop(0, steps - direct, drain, 0)
+    for at in range(steps - direct if relayed else 0, steps):
+        for k in range(1, n_col):
+            logits_copy(k, at).wait_send()
+            logits_wait(lax.rem(col + k, n_col), at)
 
 
 def average_kernel(

time: 38.6 us -> 35.7 us (0.925)
  Pallas kernels: 37.8 us -> 34.9 us
    pallas_call x1, Pallas kernels: 34.3 us -> 31.4 us  [per_device(): pl.pallas_call(functools.partial(pair_kernel, n_row, n_col, here), out_sh...]
where the time goes in v3:
time: 35.7 us; the launch traced here: 35.6 us
  Pallas kernels  34.9 us (98%)
  between operations  0.64 us (2%)
    pallas_call x1, Pallas kernels, per_device(): pl.pallas_call(functools.partial(pair_kernel, n_row, n_col, here), out_sh...  31.4 us
    pallas_call x1, Pallas kernels, per_device(): pl.pallas_call(functools.partial(average_kernel, here), out_shape=(jax.Sh...  3.55 us

profile of v3, /device:TPU:0, one launch (start us, length us, event | category | flops | bytes accessed | tf_op | source)
XLA Modules:
  0.0 35.6 jit_solution(5494289252437231832)
XLA Ops:
  0.6 31.4 %pair.1 = (f32[48,96,128]{2,1,0:T(8,128)S(1)}, f32[4,288,128]{2,1,0:T(8,128)S(1)}, f32[8,48,512]{2,1,0:T(8,128)S(1)}, f32[2,8,48,128]{3,2,1,0:T(8,128)S(1)}, bf1...) custom-call(s32[8]{0:T(128)} %seq_in.1, s32[1,48]{1,0:T(1,128)} %bitcast.11, ...), custom_call_target="tpu_custom_call" | custom-call | tf_op jit(solution)/shard_map/pair/pallas_call | solution.py:775
  32.0 3.6 %average.1 = (f32[8,48,64]{2,1,0:T(8,128)}, f32[48,96,128]{2,1,0:T(8,128)}) custom-call(f32[4,288,128]{2,1,0:T(8,128)S(1)} %get-tuple-element.9.slots, f32[384,512]{1,0:T(8,128)S(1)} %bitcast.6, f32[2,8,48,128]{3,2,1,0:T(8,128)S(1)} %get-tuple-element.11.gate_ref, bf16[8,256,256]{2,1,0:T(8,128)(2,1)S(1)} %get-tuple-element.12.value_bd, ...), custom_call_target="tpu_custom_call" | custom-call | tf_op jit(solution)/shard_map/average/pallas_call | solution.py:845

commit v4 on v3

--- a/solution.py
+++ b/solution.py
@@ -77,6 +77,7 @@
     n_row,
     n_col,
     here,
+    early,
     seq_in,
     res_in,
     align_in,
@@ -90,11 +91,13 @@
     pair_in,
     pair_out,
     slots,
-    norm_all,
+    norm_high,
+    norm_low,
     gate_out,
     value_bd,
     output_bd,
     align_ref,
+    early_out,
     seq_ref,
     res_ref,
     left_w_ref,
@@ -104,9 +107,12 @@
     value_w_ref,
     gate_w_ref,
     output_w_ref,
+    norm_all,
     rows_buf,
     masked_buf,
     block_buf,
+    block_high,
+    block_low,
     right_buf,
     left_ref,
     right_ref,
@@ -140,11 +146,11 @@
         pltpu.make_async_copy(source, target, load_sem.at[at])
         for at, (source, target) in enumerate(
             [
+                (right_w_in, right_w_ref),
+                (res_in, res_ref),
+                (left_w_in, left_w_ref),
+                (seq_in, seq_ref),
                 (align_in, align_ref),
-                (seq_in, seq_ref),
-                (res_in, res_ref),
-                (right_w_in, right_w_ref),
-                (left_w_in, left_w_ref),
                 (outer_in, outer_ref),
                 (gate_w_in, gate_w_ref),
                 (value_w_in, value_w_ref),
@@ -219,7 +225,7 @@
     if relayed:
         greeters = greeters - jnp.where((col == 0) | (col == n_col - 1), 1, 0)
     meet(greet)
-    for at in range(5):
+    for at in range(4):
         loads[at].wait()
     res_row = res_ref[...].astype(F32)
     diag = iota((rows, rows), 0) == iota((rows, rows), 1)
@@ -232,22 +238,25 @@
     res_col = column(res_row)
     spread = jnp.broadcast_to(right_w_ref[...][:, None, :], (factor, seqs, width))
     row_seq = iota((factor, seqs, width), 1)
+    for s in range(seqs):
+        block_buf[:, s * width : (s + 1) * width] = jnp.where(row_seq == s, spread, 0.0).reshape(
+            factor * seqs, width
+        )
+    wr_high, wr_low = split(block_buf[...])
+    block_high[...] = wr_high
+    block_low[...] = wr_low
+    wl_high, wl_low = split(left_w_ref[...])
+    right_buf[rows : rows + 8, 0:rows] = jnp.broadcast_to(res_row, (8, rows))
+    right_buf[rows : rows + 8, rows:] = jnp.zeros((8, right_buf.shape[1] - rows), F32)
+    loads[4].wait()
     seq_sum = 0.0
     for s in range(seqs):
         normed = layer_norm(align_ref[s])
         norm_all[row, :, s * width : (s + 1) * width] = normed
         live = seq_ref[s].astype(F32)
         seq_sum = seq_sum + live
-        masked = normed * (res_col * live)
-        masked_buf[:, s * width : (s + 1) * width] = masked
-        rows_buf[pl.ds(s, rows, stride=seqs), :] = masked
-        block_buf[:, s * width : (s + 1) * width] = jnp.where(row_seq == s, spread, 0.0).reshape(
-            factor * seqs, width
-        )
-    wr_high, wr_low = split(block_buf[...])
-    right_buf[0:rows, :] = dot_split(masked_buf[...], wr_high, wr_low, dot_t)
-    right_buf[rows : rows + 8, 0:rows] = jnp.broadcast_to(res_row, (8, rows))
-    right_buf[rows : rows + 8, rows:] = jnp.zeros((8, right_buf.shape[1] - rows), F32)
+        masked_buf[:, s * width : (s + 1) * width] = normed * (res_col * live)
+    right_buf[0:rows, :] = dot_split(masked_buf[...], block_high[...], block_low[...], dot_t)
     pl.semaphore_wait(barrier, greeters)
     turn = pltpu.make_async_remote_copy(
         right_buf,
@@ -267,7 +276,8 @@
     def _():
         stay.start()
 
-    wl_high, wl_low = split(left_w_ref[...])
+    for s in range(seqs):
+        rows_buf[pl.ds(s, rows, stride=seqs), :] = masked_buf[:, s * width : (s + 1) * width]
     left = dot_split(rows_buf[...], wl_high, wl_low, dot_t)
     for g in range(4):
         left_ref[col, 0:quarter, g * factor : (g + 1) * factor] = left[
@@ -302,8 +312,8 @@
         return pltpu.make_async_remote_copy(
             right_ref.at[row],
             right_ref.at[row],
-            right_send.at[k],
-            right_recv.at[half - k],
+            right_send,
+            right_recv.at[half - k - 1],
             device_id=(peer_row(k), col),
             device_id_type=MESH,
         )
@@ -313,8 +323,8 @@
         return pltpu.make_async_remote_copy(
             right_ref.at[src],
             right_ref.at[src],
-            share_send.at[k],
-            share_recv.at[k],
+            share_send,
+            share_recv,
             device_id=(partner, col),
             device_id_type=MESH,
         )
@@ -323,8 +333,8 @@
         return pltpu.make_async_remote_copy(
             norm_all.at[row],
             norm_all.at[row],
-            norm_send.at[k],
-            norm_recv.at[half - k],
+            norm_send,
+            norm_recv,
             device_id=(peer_row(k), col),
             device_id_type=MESH,
         )
@@ -333,8 +343,8 @@
         return pltpu.make_async_remote_copy(
             norm_all.at[peer_row(k)],
             norm_all.at[peer_row(k)],
-            relay_send.at[k],
-            relay_recv.at[k],
+            relay_send,
+            relay_recv,
             device_id=(partner, col),
             device_id_type=MESH,
         )
@@ -425,7 +435,7 @@
 
         @pl.when(k == 1)
         def _():
-            for k2 in range(1, n_col):
+            for k2 in sorted(range(1, n_col), key=lambda d: min(d, n_col - d)):
                 near(lax.rem(col + k2, n_col), left_copy(k2).start)
             prepare()
             pltpu.make_async_copy(right_buf, right_ref.at[row], turn_sem.at[1]).wait()
@@ -443,12 +453,9 @@
         def _():
             for k2 in range(1, half):
                 pltpu.make_async_copy(
-                    right_buf, right_ref.at[peer_row(k2)], right_recv.at[k2]
+                    right_buf, right_ref.at[peer_row(k2)], right_recv.at[k2 - 1]
                 ).wait()
                 share_copy(k2).start()
-            relay_copy(0).start()
-            for k2 in range(1, half):
-                norm_copy(k2).start()
 
         @pl.when(k > 0)
         def _():
@@ -461,9 +468,10 @@
         return carry
 
     lax.fori_loop(0, n_col, stage, 0)
-    for k in range(half):
-        src = 2 * lax.rem(chip + k, half) + 1 - core
-        pltpu.make_async_copy(right_buf, right_ref.at[src], share_recv.at[k]).wait()
+    def blocks(ref, number, sem):
+        pltpu.make_async_copy(ref.at[pl.ds(0, number)], ref.at[pl.ds(0, number)], sem).wait()
+
+    blocks(right_ref, half, share_recv)
     count = left_ref[0, quarter : quarter + 1, 0:1]
     for c in range(1, n_col):
         count = count + left_ref[c, quarter : quarter + 1, 0:1]
@@ -487,13 +495,23 @@
     def chunk(at):
         return pl.ds(pl.multiple_of(at * jrows, jrows), jrows)
 
+    lag, direct = 2, 2
+    first = steps - direct
+
     def logits_copy(k, at):
+        other = lax.rem(col + k, n_col)
+        sem = jnp.where(at < early, col, n_col + col)
+        if relayed:
+            passed = (at < first) & (
+                ((col == 0) & (other == n_col - 2)) | ((col == n_col - 1) & (other == 1))
+            )
+            sem = jnp.where(passed, 2 * n_col + at, sem)
         return pltpu.make_async_remote_copy(
             slots.at[col, chunk(at)],
             slots.at[col, chunk(at)],
-            logits_send.at[k, at],
-            logits_recv.at[col, at],
-            device_id=(row, lax.rem(col + k, n_col)),
+            logits_send.at[k],
+            logits_recv.at[sem],
+            device_id=(row, other),
             device_id_type=MESH,
         )
 
@@ -501,24 +519,21 @@
         return pltpu.make_async_remote_copy(
             slots.at[far_src, chunk(at)],
             slots.at[far_src, chunk(at)],
-            logits_send.at[0, at],
-            logits_recv.at[far_src, at],
+            logits_send.at[0],
+            logits_recv.at[jnp.where(at < early, far_src, n_col + far_src)],
             device_id=(row, far_dest),
             device_id_type=MESH,
         )
 
-    def logits_wait(src, at):
-        pltpu.make_async_copy(
-            slots.at[src, chunk(at)], slots.at[src, chunk(at)], logits_recv.at[src, at]
-        ).wait()
+    def chunks(src, number, sem):
+        part = slots.at[src, pl.ds(0, number * jrows)]
+        pltpu.make_async_copy(part, part, sem).wait()
 
     def pass_on(at):
         @pl.when(relay)
         def _():
-            logits_wait(far_src, at)
+            chunks(far_src, 1, logits_recv.at[2 * n_col + at])
             logits_forward(at).start()
-
-    lag, direct = 2, 1
 
     def body(step, carry):
         first_row = pl.multiple_of(step * here, here)
@@ -579,28 +594,23 @@
             def _():
                 pass_on(step - lag)
 
-        @pl.when(step == steps // 2)
+        @pl.when(step == 1)
         def _():
+            relay_copy(0).start()
             for k in range(1, half):
-                pltpu.make_async_copy(
-                    norm_all.at[row], norm_all.at[peer_row(k)], norm_recv.at[k]
-                ).wait()
-                relay_copy(k).start()
+                norm_copy(k).start()
 
         return carry
 
     lax.fori_loop(0, steps, body, 0)
     if relayed:
-        for at in range(steps - lag, steps - direct):
+        for at in range(steps - lag, first):
             pass_on(at)
-    for k in range(half):
-        other = 2 * lax.rem(chip + k, half) + 1 - core
-        pltpu.make_async_copy(norm_all.at[row], norm_all.at[other], relay_recv.at[k]).wait()
-        relay_copy(k).wait_send()
-        share_copy(k).wait_send()
+    blocks(norm_all, half - 1, norm_recv)
     for k in range(1, half):
-        norm_copy(k).wait_send()
-        right_copy(k).wait_send()
+        relay_copy(k).start()
+    blocks(right_ref, half, share_send)
+    blocks(right_ref, half - 1, right_send)
     for k in range(1, n_col):
         near(lax.rem(col + k, n_col), left_copy(k).wait_send)
 
@@ -613,53 +623,58 @@
         @pl.when(relay)
         def _():
             left_forward().wait_send()
-
-    def drain(at, carry):
-        for k in range(1, n_col):
-            other = lax.rem(col + k, n_col)
-            near(other, logits_copy(k, at).wait_send)
-            unless_relayed(other, lambda: logits_wait(other, at))
+            chunks(far_src, first, logits_send.at[0])
+
+    blocks(norm_all, half, relay_recv)
+    for r in range(n_row):
+        high, low = split(norm_all[r])
+        norm_high[r] = high
+        norm_low[r] = low
+    for k in range(1, n_col):
+        other = lax.rem(col + k, n_col)
+        unless_relayed(other, lambda: chunks(other, early, logits_recv.at[other]))
+
+    def keep(s, values):
+        early_out[s] = values
+
+    average_rows(
+        here,
+        range(early),
+        slots,
+        norm_high[...].reshape(n_row * rows, seqs * width),
+        norm_low[...].reshape(n_row * rows, seqs * width),
+        gate_out,
+        value_bd,
+        output_bd,
+        align_ref,
+        keep,
+    )
+    blocks(norm_all, half - 1, norm_send)
+    blocks(norm_all, half, relay_send)
+    for k in range(1, n_col):
+        other = lax.rem(col + k, n_col)
         if relayed:
-
-            @pl.when(relay)
-            def _():
-                logits_forward(at).wait_send()
-
-        return carry
-
-    if relayed:
-        lax.fori_loop(0, steps - direct, drain, 0)
-    for at in range(steps - direct if relayed else 0, steps):
-        for k in range(1, n_col):
-            logits_copy(k, at).wait_send()
-            logits_wait(lax.rem(col + k, n_col), at)
-
-
-def average_kernel(
-    here,
-    slots,
-    norm_ref,
-    gate_ref,
-    value_bd,
-    output_bd,
-    align_ref,
-    pair_ref,
-    out_any,
-    pair_any,
-    out_buf,
-    sems,
+            near(other, lambda: chunks(col, steps, logits_send.at[k]))
+            pl.when(is_far(other))(lambda: chunks(col, direct, logits_send.at[k]))
+        else:
+            chunks(col, steps, logits_send.at[k])
+        last = logits_recv.at[n_col + other]
+        unless_relayed(other, lambda: chunks(other, steps - early, last))
+        if relayed:
+            pl.when(relay & (other == far_src))(lambda: chunks(other, direct, last))
+
+
+def average_rows(
+    here, taken, slots, norm_high, norm_low, gate_ref, value_bd, output_bd, align_ref, store
 ):
-    place = pltpu.make_async_copy(pair_ref, pair_any, sems.at[0])
-    place.start()
     seqs, rows, width = align_ref.shape
     n_col, total_rows, _ = slots.shape
     groups, heads = gate_ref.shape[0], gate_ref.shape[1]
     group = seqs // groups
-    steps = rows // here
-    jrows = total_rows // steps
+    jrows = total_rows // (rows // here)
     wide = here * heads
     parts = LANES // wide
-    norm_high, norm_low = split(norm_ref[...])
+    own_rows = slice(taken[0] * here, (taken[-1] + 1) * here)
     part_of = iota((jrows, LANES), 1) // wide
 
     def over_parts(values, combine):
@@ -669,7 +684,7 @@
         return out
 
     weights = []
-    for t in range(steps):
+    for t in taken:
         pieces = [slots[c, t * jrows : (t + 1) * jrows, :] for c in range(n_col)]
         top = pieces[0]
         for piece in pieces[1:]:
@@ -682,7 +697,7 @@
         inverse = 1.0 / over_parts(jnp.sum(total, axis=0, keepdims=True), jnp.add)
         weights.append([piece * inverse for piece in pieces])
     turned = []
-    for t in range(0, steps, parts):
+    for t in range(0, len(taken), parts):
         blocks = []
         for c in range(n_col):
             for p in range(parts):
@@ -705,11 +720,11 @@
                         t * wide + h * here : t * wide + (h + 1) * here,
                         g * group * width : (g + 1) * group * width,
                     ]
-                    for t in range(steps)
+                    for t in range(len(taken))
                 ],
                 axis=0,
             )
-            gated.append(stacked_dot(own, value_bd[h]) * gate_ref[g, h])
+            gated.append(stacked_dot(own, value_bd[h]) * gate_ref[g, h, own_rows, :])
         out = None
         for hp in range(heads // 2):
             part = dot_split(
@@ -720,19 +735,55 @@
             out = part if out is None else out + part
         for s in range(group):
             at = g * group + s
-            out_buf[at] = align_ref[at] + out[:, s * width : (s + 1) * width]
-        pltpu.make_async_copy(
-            out_buf.at[pl.ds(g * group, group)],
-            out_any.at[pl.ds(g * group, group)],
-            sems.at[1 + g],
-        ).start()
-    for g in range(groups):
-        pltpu.make_async_copy(
-            out_buf.at[pl.ds(g * group, group)],
-            out_any.at[pl.ds(g * group, group)],
-            sems.at[1 + g],
-        ).wait()
-    place.wait()
+            store(at, align_ref[at, own_rows, :] + out[:, s * width : (s + 1) * width])
+
+
+def average_kernel(
+    here,
+    early,
+    slots,
+    norm_high,
+    norm_low,
+    gate_ref,
+    value_bd,
+    output_bd,
+    align_ref,
+    early_ref,
+    pair_ref,
+    out_any,
+    pair_any,
+    out_buf,
+    sems,
+):
+    rows = align_ref.shape[1]
+    steps = rows // here
+    first = early * here
+    copies = [
+        pltpu.make_async_copy(pair_ref, pair_any, sems.at[0]),
+        pltpu.make_async_copy(early_ref, out_any.at[:, pl.ds(0, first), :], sems.at[1]),
+        pltpu.make_async_copy(out_buf, out_any.at[:, pl.ds(first, rows - first), :], sems.at[2]),
+    ]
+    copies[0].start()
+    copies[1].start()
+
+    def keep(s, values):
+        out_buf[s] = values
+
+    average_rows(
+        here,
+        range(early, steps),
+        slots,
+        norm_high[...],
+        norm_low[...],
+        gate_ref,
+        value_bd,
+        output_bd,
+        align_ref,
+        keep,
+    )
+    copies[2].start()
+    for copy in copies:
+        copy.wait()
 
 
 def per_device(
@@ -760,6 +811,7 @@
     half = n_row // 2
     here = 8
     steps = rows // here
+    early = LANES // (here * heads)
     jrows = cols * here * heads // LANES
     group = LANES * heads // channels
     groups = seqs // group
@@ -772,19 +824,21 @@
     row_bytes = 4 * n_col * k_col * pair_width
     premixed = rows * row_bytes <= MIX_BYTES
     held = rows if premixed else here
-    pair_new, slots, norm_all, gate, value_bd, output_bd, align = pl.pallas_call(
-        functools.partial(pair_kernel, n_row, n_col, here),
+    pair_new, slots, norm_high, norm_low, gate, value_bd, output_bd, align, started = pl.pallas_call(
+        functools.partial(pair_kernel, n_row, n_col, here, early),
         out_shape=(
             pltpu.VMEM(pair_rep.shape, F32),
             pltpu.VMEM((n_col, steps * jrows, LANES), F32),
-            pltpu.VMEM((n_row, rows, seqs * width), F32),
+            pltpu.VMEM((n_row, rows, seqs * width), BF16),
+            pltpu.VMEM((n_row, rows, seqs * width), BF16),
             pltpu.VMEM((groups, heads, rows, LANES), F32),
             pltpu.VMEM((heads, group * width, 2 * LANES), BF16),
             pltpu.VMEM((2, heads // 2, 2 * LANES, group * width), BF16),
             pltpu.VMEM(alignment.shape, F32),
+            pltpu.VMEM((seqs, early * here, width), F32),
         ),
         in_specs=[anywhere] * 11,
-        out_specs=(vmem,) * 7,
+        out_specs=(vmem,) * 9,
         scratch_shapes=[
             pltpu.SMEM((seqs,), jnp.int32),
             pltpu.VMEM((1, rows), jnp.int32),
@@ -795,9 +849,12 @@
             pltpu.VMEM(value_weight.shape, F32),
             pltpu.VMEM(gate_weight.shape, F32),
             pltpu.VMEM((width, channels), F32),
+            pltpu.VMEM((n_row, rows, seqs * width), F32),
             pltpu.VMEM((rows * seqs, width), F32),
             pltpu.VMEM((rows, seqs * width), F32),
             pltpu.VMEM((k_col, seqs * width), F32),
+            pltpu.VMEM((k_col, seqs * width), BF16),
+            pltpu.VMEM((k_col, seqs * width), BF16),
             pltpu.VMEM(right_shape, F32),
             pltpu.VMEM((n_col,) + left_shape, F32),
             pltpu.VMEM((n_row,) + right_shape, F32),
@@ -814,16 +871,16 @@
             dma((n_col,)),
             dma((n_col,)),
             dma((2,)),
-            dma((half,)),
-            dma((half,)),
-            dma((half,)),
-            dma((half,)),
-            dma((n_col, steps)),
-            dma((n_col, steps)),
-            dma((half,)),
-            dma((half,)),
-            dma((half,)),
-            dma((half,)),
+            dma,
+            dma((half - 1,)),
+            dma,
+            dma,
+            dma((n_col,)),
+            dma((2 * n_col + steps,)),
+            dma,
+            dma,
+            dma,
+            dma,
         ],
         compiler_params=pltpu.CompilerParams(
             collective_id=0, has_side_effects=True, vmem_limit_bytes=PAIR_VMEM
@@ -843,23 +900,25 @@
         pair_rep,
     )
     alignment_out, pair_final = pl.pallas_call(
-        functools.partial(average_kernel, here),
+        functools.partial(average_kernel, here, early),
         out_shape=(
             jax.ShapeDtypeStruct(alignment.shape, F32),
             jax.ShapeDtypeStruct(pair_rep.shape, F32),
         ),
-        in_specs=[vmem] * 7,
+        in_specs=[vmem] * 9,
         out_specs=(anywhere, anywhere),
-        scratch_shapes=[pltpu.VMEM(alignment.shape, F32), dma((1 + groups,))],
+        scratch_shapes=[pltpu.VMEM((seqs, (steps - early) * here, width), F32), dma((3,))],
         compiler_params=pltpu.CompilerParams(vmem_limit_bytes=AVERAGE_VMEM),
         name="average",
     )(
         slots,
-        norm_all.reshape(n_row * rows, seqs * width),
+        norm_high.reshape(n_row * rows, seqs * width),
+        norm_low.reshape(n_row * rows, seqs * width),
         gate,
         value_bd,
         output_bd,
         align,
+        started,
         pair_new,
     )
     return (alignment_out, pair_final)

time: 35.7 us -> 34.4 us (0.964)
  Pallas kernels: 34.9 us -> 33.6 us
    pallas_call x2, Pallas kernels: 34.9 us -> 33.6 us  [the longest x1 30.7 us: per_device(): pl.pallas_call(functools.partial(pair_kernel, n_row, n_col, here, early),...]
where the time goes in v4:
time: 34.4 us; the launch traced here: 34.2 us
  Pallas kernels  33.6 us (98%)
  between operations  0.64 us (2%)
    pallas_call x1, Pallas kernels, per_device(): pl.pallas_call(functools.partial(pair_kernel, n_row, n_col, here, early),...  30.7 us
    pallas_call x1, Pallas kernels, per_device(): pl.pallas_call(functools.partial(average_kernel, here, early), out_shape=...  2.91 us

profile of v4, /device:TPU:0, one launch (start us, length us, event | category | flops | bytes accessed | tf_op | source)
XLA Modules:
  0.0 34.2 jit_solution(15071502080682188457)
XLA Ops:
  0.6 30.7 %pair.1 = (f32[48,96,128]{2,1,0:T(8,128)S(1)}, f32[4,288,128]{2,1,0:T(8,128)S(1)}, bf16[8,48,512]{2,1,0:T(8,128)(2,1)S(1)}, bf16[8,48,512]{2,1,0:T(8,128)(2,1)S(...) custom-call(s32[8]{0:T(128)} %seq_in.1, ...), custom_call_target="tpu_custom_call" | custom-call | tf_op jit(solution)/shard_map/pair/pallas_call | solution.py:827
  31.3 2.9 %average.1 = (f32[8,48,64]{2,1,0:T(8,128)}, f32[48,96,128]{2,1,0:T(8,128)}) custom-call(f32[4,288,128]{2,1,0:T(8,128)S(1)} %get-tuple-element.11.slots, bf16[384,512]{1,0:T(8,128)(2,1)S(1)} %bitcast.7, bf16[384,512]{1,0:T(8,128)(2,1)S(1)} %bitcast.8, f32[2,8,48,128]{3,2,1,0:T(8,128)S(1)} %get-tuple-element.14.gate_ref, ...), custom_call_target="tpu_custom_call" | custom-call | tf_op jit(solution)/shard_map/average/pallas_call | solution.py:902

commit v5 on v4

--- a/solution.py
+++ b/solution.py
@@ -91,6 +91,7 @@
     pair_in,
     pair_out,
     slots,
+    mask_out,
     norm_high,
     norm_low,
     gate_out,
@@ -121,7 +122,6 @@
     w_buf,
     l_buf,
     r_buf,
-    mask_buf,
     high_buf,
     low_buf,
     pair_ref,
@@ -246,17 +246,17 @@
     block_high[...] = wr_high
     block_low[...] = wr_low
     wl_high, wl_low = split(left_w_ref[...])
-    right_buf[rows : rows + 8, 0:rows] = jnp.broadcast_to(res_row, (8, rows))
-    right_buf[rows : rows + 8, rows:] = jnp.zeros((8, right_buf.shape[1] - rows), F32)
+    norm_all[row, rows : rows + 8, 0:rows] = jnp.broadcast_to(res_row, (8, rows))
+    norm_all[row, rows : rows + 8, rows:] = jnp.zeros((8, seqs * width - rows), F32)
     loads[4].wait()
     seq_sum = 0.0
     for s in range(seqs):
         normed = layer_norm(align_ref[s])
-        norm_all[row, :, s * width : (s + 1) * width] = normed
+        norm_all[row, 0:rows, s * width : (s + 1) * width] = normed
         live = seq_ref[s].astype(F32)
         seq_sum = seq_sum + live
         masked_buf[:, s * width : (s + 1) * width] = normed * (res_col * live)
-    right_buf[0:rows, :] = dot_split(masked_buf[...], block_high[...], block_low[...], dot_t)
+    right_buf[...] = dot_split(masked_buf[...], block_high[...], block_low[...], dot_t)
     pl.semaphore_wait(barrier, greeters)
     turn = pltpu.make_async_remote_copy(
         right_buf,
@@ -394,10 +394,18 @@
 
         spread_heads(gate_w_ref[...], heads, group, keep_gate)
         spread_heads(value_w_ref[...], heads, group, keep_value)
-        for g in range(seqs // group):
-            own = norm_all[row, :, g * group * width : (g + 1) * group * width]
-            for h in range(heads):
-                gate_out[g, h] = jax.nn.sigmoid(stacked_dot(own, gate_bd[h]))
+        groups = seqs // group
+        own = jnp.concatenate(
+            [
+                norm_all[row, 0:rows, g * group * width : (g + 1) * group * width]
+                for g in range(groups)
+            ],
+            axis=0,
+        )
+        for h in range(heads):
+            gate = jax.nn.sigmoid(stacked_dot(own, gate_bd[h]))
+            for g in range(groups):
+                gate_out[g, h] = gate[g * rows : (g + 1) * rows]
         channels = output_w_ref.shape[1]
         head_width = channels // heads
         lanes = iota((width, group * width), 1)
@@ -439,7 +447,10 @@
                 near(lax.rem(col + k2, n_col), left_copy(k2).start)
             prepare()
             pltpu.make_async_copy(right_buf, right_ref.at[row], turn_sem.at[1]).wait()
-            for k2 in range(1, half):
+            odd = lax.rem(chip, 2)
+            right_copy(half - 1 - odd * (half - 2)).start()
+            right_copy(1 + odd * (half - 2)).start()
+            for k2 in range(2, half - 1):
                 right_copy(k2).start()
             share_copy(0).start()
             if relayed:
@@ -478,19 +489,11 @@
     scale = 1.0 / jnp.maximum(count, 1.0)
     for c in range(n_col):
         for t in range(ratio):
-            high_r, low_r = split(right_ref[c * ratio + t, 0:rows, :])
+            high_r, low_r = split(right_ref[c * ratio + t])
             lanes = slice(c * k_col, (c + 1) * k_col)
             r_buf[t * rows : (t + 1) * rows, lanes] = high_r
             r_buf[cols + t * rows : cols + (t + 1) * rows, lanes] = low_r
-    res_cols = jnp.concatenate(
-        [column(right_ref[t, rows : rows + 1, 0:rows]) for t in range(ratio)], axis=0
-    )
     part_of = iota((jrows, LANES), 1) // (here * heads)
-    mask = jnp.zeros((jrows, LANES), F32)
-    for p in range(parts):
-        dead = (res_cols[p * jrows : (p + 1) * jrows] - 1.0) * 1000000000.0
-        mask = jnp.where(part_of == p, dead, mask)
-    mask_buf[...] = mask
 
     def chunk(at):
         return pl.ds(pl.multiple_of(at * jrows, jrows), jrows)
@@ -548,8 +551,8 @@
                 [high_buf[i].reshape(depth, pair_width) for i in at], axis=1
             )
             right_low = jnp.concatenate([low_buf[i].reshape(depth, pair_width) for i in at], axis=1)
-            first = dot(r_both, right_high)
-            sums = first[:cols] + (first[cols:] + dot(r_both[:cols], right_low))
+            product = dot(r_both, right_high)
+            sums = product[:cols] + (product[cols:] + dot(r_both[:cols], right_low))
             for t in range(2):
                 i = first_row + 2 * p + t
                 pair_out[i] = pair_ref[i] + sums[:, t * pair_width : (t + 1) * pair_width] * scale
@@ -579,7 +582,7 @@
         logits = total[:jrows]
         for p in range(1, parts):
             logits = jnp.where(part_of == p, total[p * jrows : (p + 1) * jrows], logits)
-        slots[col, chunk(step), :] = logits + mask_buf[...]
+        slots[col, chunk(step), :] = logits
         for k in range(1, n_col):
             other = lax.rem(col + k, n_col)
             if relayed:
@@ -627,9 +630,19 @@
 
     blocks(norm_all, half, relay_recv)
     for r in range(n_row):
-        high, low = split(norm_all[r])
+        high, low = split(norm_all[r, 0:rows, :])
         norm_high[r] = high
         norm_low[r] = low
+    for c in range(n_col):
+        res_cols = jnp.concatenate(
+            [column(norm_all[c * ratio + t, rows : rows + 1, 0:rows]) for t in range(ratio)],
+            axis=0,
+        )
+        mask = jnp.zeros((jrows, LANES), F32)
+        for p in range(parts):
+            dead = (res_cols[p * jrows : (p + 1) * jrows] - 1.0) * 1000000000.0
+            mask = jnp.where(part_of == p, dead, mask)
+        mask_out[c] = mask
     for k in range(1, n_col):
         other = lax.rem(col + k, n_col)
         unless_relayed(other, lambda: chunks(other, early, logits_recv.at[other]))
@@ -641,6 +654,7 @@
         here,
         range(early),
         slots,
+        mask_out,
         norm_high[...].reshape(n_row * rows, seqs * width),
         norm_low[...].reshape(n_row * rows, seqs * width),
         gate_out,
@@ -665,7 +679,7 @@
 
 
 def average_rows(
-    here, taken, slots, norm_high, norm_low, gate_ref, value_bd, output_bd, align_ref, store
+    here, taken, slots, mask_ref, norm_high, norm_low, gate_ref, value_bd, output_bd, align_ref, store
 ):
     seqs, rows, width = align_ref.shape
     n_col, total_rows, _ = slots.shape
@@ -685,7 +699,9 @@
 
     weights = []
     for t in taken:
-        pieces = [slots[c, t * jrows : (t + 1) * jrows, :] for c in range(n_col)]
+        pieces = [
+            slots[c, t * jrows : (t + 1) * jrows, :] + mask_ref[c] for c in range(n_col)
+        ]
         top = pieces[0]
         for piece in pieces[1:]:
             top = jnp.maximum(top, piece)
@@ -711,37 +727,42 @@
                 blocks.append(block)
         turned.append(jnp.concatenate(blocks, axis=0).T)
     mixed = dot_split(jnp.concatenate(turned, axis=0), norm_high, norm_low)
+    count = len(taken) * here
+    gated = []
+    for h in range(heads):
+        own = jnp.concatenate(
+            [
+                mixed[
+                    t * wide + h * here : t * wide + (h + 1) * here,
+                    g * group * width : (g + 1) * group * width,
+                ]
+                for g in range(groups)
+                for t in range(len(taken))
+            ],
+            axis=0,
+        )
+        gate = jnp.concatenate([gate_ref[g, h, own_rows, :] for g in range(groups)], axis=0)
+        gated.append(stacked_dot(own, value_bd[h]) * gate)
+    out = None
+    for hp in range(heads // 2):
+        part = dot_split(
+            jnp.concatenate(gated[2 * hp : 2 * hp + 2], axis=1),
+            output_bd[0, hp],
+            output_bd[1, hp],
+        )
+        out = part if out is None else out + part
     for g in range(groups):
-        gated = []
-        for h in range(heads):
-            own = jnp.concatenate(
-                [
-                    mixed[
-                        t * wide + h * here : t * wide + (h + 1) * here,
-                        g * group * width : (g + 1) * group * width,
-                    ]
-                    for t in range(len(taken))
-                ],
-                axis=0,
-            )
-            gated.append(stacked_dot(own, value_bd[h]) * gate_ref[g, h, own_rows, :])
-        out = None
-        for hp in range(heads // 2):
-            part = dot_split(
-                jnp.concatenate(gated[2 * hp : 2 * hp + 2], axis=1),
-                output_bd[0, hp],
-                output_bd[1, hp],
-            )
-            out = part if out is None else out + part
         for s in range(group):
             at = g * group + s
-            store(at, align_ref[at, own_rows, :] + out[:, s * width : (s + 1) * width])
+            change = out[g * count : (g + 1) * count, s * width : (s + 1) * width]
+            store(at, align_ref[at, own_rows, :] + change)
 
 
 def average_kernel(
     here,
     early,
     slots,
+    mask_ref,
     norm_high,
     norm_low,
     gate_ref,
@@ -773,6 +794,7 @@
         here,
         range(early, steps),
         slots,
+        mask_ref,
         norm_high[...],
         norm_low[...],
         gate_ref,
@@ -819,16 +841,17 @@
     anywhere = pl.BlockSpec(memory_space=pl.ANY)
     dma = pltpu.SemaphoreType.DMA
     left_shape = (quarter + 8, 4 * factor)
-    right_shape = (rows + 8, k_col)
+    right_shape = (rows, k_col)
     mix_row = (n_col, factor // 2, 2 * seqs, pair_width)
     row_bytes = 4 * n_col * k_col * pair_width
     premixed = rows * row_bytes <= MIX_BYTES
     held = rows if premixed else here
-    pair_new, slots, norm_high, norm_low, gate, value_bd, output_bd, align, started = pl.pallas_call(
+    pair_new, slots, mask, norm_high, norm_low, gate, value_bd, output_bd, align, started = pl.pallas_call(
         functools.partial(pair_kernel, n_row, n_col, here, early),
         out_shape=(
             pltpu.VMEM(pair_rep.shape, F32),
             pltpu.VMEM((n_col, steps * jrows, LANES), F32),
+            pltpu.VMEM((n_col, jrows, LANES), F32),
             pltpu.VMEM((n_row, rows, seqs * width), BF16),
             pltpu.VMEM((n_row, rows, seqs * width), BF16),
             pltpu.VMEM((groups, heads, rows, LANES), F32),
@@ -838,7 +861,7 @@
             pltpu.VMEM((seqs, early * here, width), F32),
         ),
         in_specs=[anywhere] * 11,
-        out_specs=(vmem,) * 9,
+        out_specs=(vmem,) * 10,
         scratch_shapes=[
             pltpu.SMEM((seqs,), jnp.int32),
             pltpu.VMEM((1, rows), jnp.int32),
@@ -849,7 +872,7 @@
             pltpu.VMEM(value_weight.shape, F32),
             pltpu.VMEM(gate_weight.shape, F32),
             pltpu.VMEM((width, channels), F32),
-            pltpu.VMEM((n_row, rows, seqs * width), F32),
+            pltpu.VMEM((n_row, rows + 8, seqs * width), F32),
             pltpu.VMEM((rows * seqs, width), F32),
             pltpu.VMEM((rows, seqs * width), F32),
             pltpu.VMEM((k_col, seqs * width), F32),
@@ -863,7 +886,6 @@
             pltpu.VMEM((3 * factor, factor * pair_width), BF16),
             pltpu.VMEM((1 if premixed else n_col, rows * seqs, 3 * factor), BF16),
             pltpu.VMEM((2 * cols, n_col * k_col), BF16),
-            pltpu.VMEM((jrows, LANES), F32),
             pltpu.VMEM((held,) + mix_row, BF16),
             pltpu.VMEM((held,) + mix_row, BF16),
             pltpu.VMEM(pair_rep.shape, F32),
@@ -905,13 +927,14 @@
             jax.ShapeDtypeStruct(alignment.shape, F32),
             jax.ShapeDtypeStruct(pair_rep.shape, F32),
         ),
-        in_specs=[vmem] * 9,
+        in_specs=[vmem] * 10,
         out_specs=(anywhere, anywhere),
         scratch_shapes=[pltpu.VMEM((seqs, (steps - early) * here, width), F32), dma((3,))],
         compiler_params=pltpu.CompilerParams(vmem_limit_bytes=AVERAGE_VMEM),
         name="average",
     )(
         slots,
+        mask,
         norm_high.reshape(n_row * rows, seqs * width),
         norm_low.reshape(n_row * rows, seqs * width),
         gate,

time: 34.4 us -> 33.1 us (0.962)
  Pallas kernels: 33.6 us -> 32.2 us
    pallas_call x1, Pallas kernels: 30.7 us -> 29.6 us  [per_device(): pl.pallas_call(functools.partial(pair_kernel, n_row, n_col, here, early),...]
where the time goes in v5:
time: 33.1 us; the launch traced here: 32.9 us
  Pallas kernels  32.2 us (97%)
  between operations  0.64 us (2%)
    pallas_call x1, Pallas kernels, per_device(): pl.pallas_call(functools.partial(pair_kernel, n_row, n_col, here, early),...  29.6 us
    pallas_call x1, Pallas kernels, per_device(): pl.pallas_call(functools.partial(average_kernel, here, early), out_shape=...  2.58 us

profile of v5, /device:TPU:0, one launch (start us, length us, event | category | flops | bytes accessed | tf_op | source)
XLA Modules:
  0.0 32.9 jit_solution(15724554020153658135)
XLA Ops:
  0.6 29.6 %pair.1 = (f32[48,96,128]{2,1,0:T(8,128)S(1)}, f32[4,288,128]{2,1,0:T(8,128)S(1)}, f32[4,48,128]{2,1,0:T(8,128)S(1)}, bf16[8,48,512]{2,1,0:T(8,128)(2,1)S(1)}, b...) custom-call(s32[8]{0:T(128)} %seq_in.1, ...), custom_call_target="tpu_custom_call" | custom-call | tf_op jit(solution)/shard_map/pair/pallas_call | solution.py:849
  30.3 2.6 %average.1 = (f32[8,48,64]{2,1,0:T(8,128)}, f32[48,96,128]{2,1,0:T(8,128)}) custom-call(f32[4,288,128]{2,1,0:T(8,128)S(1)} %get-tuple-element.12.slots, f32[4,48,128]{2,1,0:T(8,128)S(1)} %get-tuple-element.13.mask_ref, bf16[384,512]{1,0:T(8,128)(2,1)S(1)} %bitcast.7, bf16[384,512]{1,0:T(8,128)(2,1)S(1)} %bitcast.8, ...), custom_call_target="tpu_custom_call" | custom-call | tf_op jit(solution)/shard_map/average/pallas_call | solution.py:924

commit v6 on v5

--- a/solution.py
+++ b/solution.py
@@ -498,7 +498,7 @@
     def chunk(at):
         return pl.ds(pl.multiple_of(at * jrows, jrows), jrows)
 
-    lag, direct = 2, 2
+    lag, direct = 2, 1
     first = steps - direct
 
     def logits_copy(k, at):
@@ -597,37 +597,21 @@
             def _():
                 pass_on(step - lag)
 
-        @pl.when(step == 1)
+        @pl.when(step == steps - 2)
         def _():
-            relay_copy(0).start()
+            blocks(norm_all, half - 1, norm_recv)
             for k in range(1, half):
-                norm_copy(k).start()
+                relay_copy(k).start()
 
         return carry
 
+    relay_copy(0).start()
+    for k in range(1, half):
+        norm_copy(k).start()
     lax.fori_loop(0, steps, body, 0)
     if relayed:
         for at in range(steps - lag, first):
             pass_on(at)
-    blocks(norm_all, half - 1, norm_recv)
-    for k in range(1, half):
-        relay_copy(k).start()
-    blocks(right_ref, half, share_send)
-    blocks(right_ref, half - 1, right_send)
-    for k in range(1, n_col):
-        near(lax.rem(col + k, n_col), left_copy(k).wait_send)
-
-    @pl.when(away)
-    def _():
-        turn.wait_send()
-
-    if relayed:
-
-        @pl.when(relay)
-        def _():
-            left_forward().wait_send()
-            chunks(far_src, first, logits_send.at[0])
-
     blocks(norm_all, half, relay_recv)
     for r in range(n_row):
         high, low = split(norm_all[r, 0:rows, :])
@@ -663,6 +647,22 @@
         align_ref,
         keep,
     )
+    blocks(right_ref, half, share_send)
+    blocks(right_ref, half - 1, right_send)
+    for k in range(1, n_col):
+        near(lax.rem(col + k, n_col), left_copy(k).wait_send)
+
+    @pl.when(away)
+    def _():
+        turn.wait_send()
+
+    if relayed:
+
+        @pl.when(relay)
+        def _():
+            left_forward().wait_send()
+            chunks(far_src, first, logits_send.at[0])
+
     blocks(norm_all, half - 1, norm_send)
     blocks(norm_all, half, relay_send)
     for k in range(1, n_col):

time: 33.1 us -> 32.8 us (level)
    pallas_call x1, Pallas kernels: 29.6 us -> 29.3 us  [per_device(): pl.pallas_call(functools.partial(pair_kernel, n_row, n_col, here, early),...]
where the time goes in v6:
time: 32.8 us; the launch traced here: 32.5 us
  Pallas kernels  31.9 us (97%)
  between operations  0.64 us (2%)
    pallas_call x1, Pallas kernels, per_device(): pl.pallas_call(functools.partial(pair_kernel, n_row, n_col, here, early),...  29.3 us
    pallas_call x1, Pallas kernels, per_device(): pl.pallas_call(functools.partial(average_kernel, here, early), out_shape=...  2.58 us

profile of v6, /device:TPU:0, one launch (start us, length us, event | category | flops | bytes accessed | tf_op | source)
XLA Modules:
  0.0 32.5 jit_solution(18191394593420144682)
XLA Ops:
  0.6 29.3 %pair.1 = (f32[48,96,128]{2,1,0:T(8,128)S(1)}, f32[4,288,128]{2,1,0:T(8,128)S(1)}, f32[4,48,128]{2,1,0:T(8,128)S(1)}, bf16[8,48,512]{2,1,0:T(8,128)(2,1)S(1)}, b...) custom-call(s32[8]{0:T(128)} %seq_in.1, ...), custom_call_target="tpu_custom_call" | custom-call | tf_op jit(solution)/shard_map/pair/pallas_call | solution.py:849
  29.9 2.6 %average.1 = (f32[8,48,64]{2,1,0:T(8,128)}, f32[48,96,128]{2,1,0:T(8,128)}) custom-call(f32[4,288,128]{2,1,0:T(8,128)S(1)} %get-tuple-element.12.slots, f32[4,48,128]{2,1,0:T(8,128)S(1)} %get-tuple-element.13.mask_ref, bf16[384,512]{1,0:T(8,128)(2,1)S(1)} %bitcast.7, bf16[384,512]{1,0:T(8,128)(2,1)S(1)} %bitcast.8, ...), custom_call_target="tpu_custom_call" | custom-call | tf_op jit(solution)/shard_map/average/pallas_call | solution.py:924

commit v7 on v6

--- a/solution.py
+++ b/solution.py
@@ -41,8 +41,10 @@
 
 
 def dot_split(left, right_high, right_low, multiply=dot):
+    count = left.shape[0]
     high, low = split(left)
-    return multiply(high, right_high) + (multiply(low, right_high) + multiply(high, right_low))
+    both = multiply(jnp.concatenate([high, low], axis=0), right_high)
+    return both[:count] + (both[count:] + multiply(high, right_low))
 
 
 def iota(shape, axis):

time: 32.8 us -> 32.8 us (level)
  no operation moved by 1% of the time
where the time goes in v7:
time: 32.8 us; the launch traced here: 32.6 us
  Pallas kernels  32 us (98%)
  between operations  0.64 us (2%)
    pallas_call x1, Pallas kernels, per_device(): pl.pallas_call(functools.partial(pair_kernel, n_row, n_col, here, early),...  29.2 us
    pallas_call x1, Pallas kernels, per_device(): pl.pallas_call(functools.partial(average_kernel, here, early), out_shape=...  2.75 us

profile of v7, /device:TPU:0, one launch (start us, length us, event | category | flops | bytes accessed | tf_op | source)
XLA Modules:
  0.0 32.6 jit_solution(7810918761972249365)
XLA Ops:
  0.6 29.2 %pair.1 = (f32[48,96,128]{2,1,0:T(8,128)S(1)}, f32[4,288,128]{2,1,0:T(8,128)S(1)}, f32[4,48,128]{2,1,0:T(8,128)S(1)}, bf16[8,48,512]{2,1,0:T(8,128)(2,1)S(1)}, b...) custom-call(s32[8]{0:T(128)} %seq_in.1, ...), custom_call_target="tpu_custom_call" | custom-call | tf_op jit(solution)/shard_map/pair/pallas_call | solution.py:851
  29.9 2.8 %average.1 = (f32[8,48,64]{2,1,0:T(8,128)}, f32[48,96,128]{2,1,0:T(8,128)}) custom-call(f32[4,288,128]{2,1,0:T(8,128)S(1)} %get-tuple-element.12.slots, f32[4,48,128]{2,1,0:T(8,128)S(1)} %get-tuple-element.13.mask_ref, bf16[384,512]{1,0:T(8,128)(2,1)S(1)} %bitcast.7, bf16[384,512]{1,0:T(8,128)(2,1)S(1)} %bitcast.8, ...), custom_call_target="tpu_custom_call" | custom-call | tf_op jit(solution)/shard_map/average/pallas_call | solution.py:926

commit v8 on v6

--- a/solution.py
+++ b/solution.py
@@ -557,7 +557,7 @@
                 i = first_row + 2 * p + t
                 pair_out[i] = pair_ref[i] + sums[:, t * pair_width : (t + 1) * pair_width] * scale
         total = None
-        batch = here // 2
+        batch = here
         for g in range(0, here, batch):
             pairs = pair_out[pl.ds(first_row + g, batch)].reshape(batch * cols, pair_width)
             high, low = split(layer_norm(pairs))

time: 32.8 us -> 32.8 us (level)
  no operation moved by 1% of the time
where the time goes in v8:
time: 32.8 us; the launch traced here: 32.5 us
  Pallas kernels  31.9 us (97%)
  between operations  0.64 us (2%)
    pallas_call x1, Pallas kernels, per_device(): pl.pallas_call(functools.partial(pair_kernel, n_row, n_col, here, early),...  29.3 us
    pallas_call x1, Pallas kernels, per_device(): pl.pallas_call(functools.partial(average_kernel, here, early), out_shape=...  2.58 us

profile of v8, /device:TPU:0, one launch (start us, length us, event | category | flops | bytes accessed | tf_op | source)
XLA Modules:
  0.0 32.5 jit_solution(18191394593420144682)
XLA Ops:
  0.6 29.3 %pair.1 = (f32[48,96,128]{2,1,0:T(8,128)S(1)}, f32[4,288,128]{2,1,0:T(8,128)S(1)}, f32[4,48,128]{2,1,0:T(8,128)S(1)}, bf16[8,48,512]{2,1,0:T(8,128)(2,1)S(1)}, b...) custom-call(s32[8]{0:T(128)} %seq_in.1, ...), custom_call_target="tpu_custom_call" | custom-call | tf_op jit(solution)/shard_map/pair/pallas_call | solution.py:849
  29.9 2.6 %average.1 = (f32[8,48,64]{2,1,0:T(8,128)}, f32[48,96,128]{2,1,0:T(8,128)}) custom-call(f32[4,288,128]{2,1,0:T(8,128)S(1)} %get-tuple-element.12.slots, f32[4,48,128]{2,1,0:T(8,128)S(1)} %get-tuple-element.13.mask_ref, bf16[384,512]{1,0:T(8,128)(2,1)S(1)} %bitcast.7, bf16[384,512]{1,0:T(8,128)(2,1)S(1)} %bitcast.8, ...), custom_call_target="tpu_custom_call" | custom-call | tf_op jit(solution)/shard_map/average/pallas_call | solution.py:924
